TPU v7x, 32 devices: a whole 2x2x4 slice. The times are simulated.
32 devices in a mesh: bx: 8 (over z, y), by: 4 (over x, core).
Axes of the slice: x: 2, y: 2, z: 4, core: 2. Of those that a mesh axis runs over, the one named last changes fastest.
Arguments:
- jitter: float32 [8, 4, 2, 256], P('bx', 'by'), may hold values from 0 to 1
- noise_var: float32 [8, 4, 256], P('bx', 'by'), may hold values from 0.5 to 2
- bases: float32 [8, 4, 2, 128, 128], P('bx', 'by'), may hold values from -0.5 to 1.5, as said below
Outputs:
- interior_factor: float32 [8, 4, 128, 128], P('bx', 'by')
- panel: float32 [8, 4, 128, 128], P('bx', 'by')
- couplings: float32 [8, 4, 8, 128, 128], P('bx', 'by')
- parent_factor: float32 [8, 4, 96, 384], P('bx', 'by')
- parent_panel: float32 [8, 4, 96, 128], P('bx', 'by')
- top_factor: float32 [8, 4, 24, 384], P('bx', 'by')
- top_panel: float32 [8, 4, 24, 128], P('bx', 'by')
- top_schur: float32 [8, 4, 8, 128], P('bx', 'by')
Inputs may be any that keep to these rules, and one draw needn't show every extreme that they name: `bases`: each of a box's two basis blocks is nonsingular.
All inputs are finite; a program needn't handle non-finite values.
Results may differ from a plain program's by a relative error of at most 0.0003.
Values sent between devices are 32-bit elements; how exact they have to be, the bound alone decides.
A program may use at most 64 MiB of HBM per device.

v0:
```python
import math

import jax
import jax.numpy as jnp
import numpy as np
from jax import lax
from jax.experimental import pallas as pl
from jax.experimental.pallas import tpu as pltpu
from jax.sharding import PartitionSpec as P

RIM = 0.125
OFFSETS = ((-1, -1), (-1, 0), (-1, 1), (0, -1), (0, 1), (1, -1), (1, 0), (1, 1))
PANEL = 64
F32 = jnp.float32


def highest(left, right):
    return jnp.dot(left, right, precision=lax.Precision.HIGHEST, preferred_element_type=F32)


def eliminate_block(block, rhs, panel=PANEL):
    size = block.shape[0]
    rows_a = [block[8 * i : 8 * i + 8] for i in range(size // 8)]
    rows_r = [rhs[8 * i : 8 * i + 8] for i in range(size // 8)]
    sub = lax.broadcasted_iota(jnp.int32, rows_a[0].shape, 0)
    for start in range(0, size, panel):
        stop = min(start + panel, size)
        first, last = start // 8, stop // 8
        for g in range(first, last):
            span = range(g, last)
            cols = {
                (m, i): jnp.broadcast_to(
                    rows_a[i][:, 8 * g + m : 8 * g + m + 1], rows_a[i].shape
                )
                for i in span
                for m in range(8)
            }
            for j in range(8):

                def row(value):
                    return jnp.broadcast_to(value[j : j + 1], value.shape)

                inv = lax.rsqrt(row(cols[j, g]))
                u_a = row(rows_a[g]) * inv
                u_r = row(rows_r[g]) * inv
                u_c = {m: row(cols[m, g]) * inv for m in range(j + 1, 8)}
                for i in span:
                    mult = cols[j, i] * inv
                    for m in range(j + 1, 8):
                        cols[m, i] = cols[m, i] - mult * u_c[m]
                    if i == g:
                        below = jnp.where(sub > j, mult, 0.0)
                        rows_a[i] = jnp.where(sub == j, u_a, rows_a[i] - below * u_a)
                        rows_r[i] = jnp.where(sub == j, u_r, rows_r[i] - below * u_r)
                    else:
                        rows_a[i] = rows_a[i] - mult * u_a
                        rows_r[i] = rows_r[i] - mult * u_r
        if stop < size:
            done_a = jnp.concatenate(rows_a[first:last], axis=0)
            done_r = jnp.concatenate(rows_r[first:last], axis=0)
            change = highest(done_a.T[stop:], jnp.concatenate([done_a, done_r], axis=1))
            for i in range(last, size // 8):
                off = 8 * i - stop
                rows_a[i] = rows_a[i] - change[off : off + 8, :size]
                rows_r[i] = rows_r[i] - change[off : off + 8, size:]
    upper = jnp.concatenate(rows_a, axis=0)
    row_id = lax.broadcasted_iota(jnp.int32, upper.shape, 0)
    col_id = lax.broadcasted_iota(jnp.int32, upper.shape, 1)
    return jnp.where(row_id <= col_id, upper, 0.0), jnp.concatenate(rows_r, axis=0)


def identity(size):
    row_id = lax.broadcasted_iota(jnp.int32, (size, size), 0)
    col_id = lax.broadcasted_iota(jnp.int32, (size, size), 1)
    return jnp.where(row_id == col_id, 1.0, 0.0).astype(F32)


def point_table(count):
    ids = np.arange(count)
    side = 2 * math.isqrt(count // 2)
    within = ids % (count // 4)
    table = np.zeros((8, count), np.float32)
    table[0] = ids // side
    table[1] = ids % side
    table[2] = within % (count // 8)
    table[3] = within // (count // 8)
    table[4] = ids // (count // 4)
    return table


def interior_points(shifts, table):
    side = math.isqrt(shifts.shape[-1] // 2)
    pos_x = RIM + (table[0:1] + shifts[0:1]) * ((1.0 - 2.0 * RIM) / side)
    pos_y = RIM + (table[1:2] + shifts[1:2]) * ((1.0 - 2.0 * RIM) / (2 * side))
    return pos_x, pos_y


def cycle_points(shifts, table):
    along = (table[2:3] + shifts[0:1]) / (shifts.shape[-1] // 8)
    depth = (table[3:4] + shifts[1:2]) * (0.5 * RIM)
    strip = table[4:5]
    pos_x = jnp.where(strip == 2.0, depth, jnp.where(strip == 3.0, 1.0 - depth, along))
    pos_y = jnp.where(strip == 0.0, depth, jnp.where(strip == 1.0, 1.0 - depth, along))
    return pos_x, pos_y


def column(row_value):
    size = row_value.shape[1]
    return jnp.broadcast_to(row_value, (size, size)).T


def wendland(first_x, first_y, second_x, second_y):
    gap_x = first_x - second_x
    gap_y = first_y - second_y
    radius = jnp.sqrt(gap_x * gap_x + gap_y * gap_y) / RIM
    inside = jnp.maximum(1.0 - radius, 0.0)
    return inside * inside * inside * inside * (4.0 * radius + 1.0)


def place():
    return lax.axis_index("bx"), lax.axis_index("by")


def send(source, target, send_sem, recv_sem, device):
    return pltpu.make_async_remote_copy(
        src_ref=source,
        dst_ref=target,
        send_sem=send_sem,
        recv_sem=recv_sem,
        device_id=device,
        device_id_type=pl.DeviceIdType.MESH,
    )


def front_kernel(jitter, noise, bases, table_ref, rotated, near_basis, near_shift, sends, recvs):
    size = bases.shape[-1]
    index_x, index_y = place()
    last_x, last_y = lax.axis_size("bx") - 1, lax.axis_size("by") - 1
    have_x = {0: index_x > 0, 1: index_x >= 0, 2: index_x < last_x}
    have_y = {0: index_y > 0, 2: index_y < last_y}
    count = jnp.int32(0)
    barrier = pltpu.get_barrier_semaphore()
    for i in (0, 2):

        @pl.when(jnp.logical_not(have_x[i]))
        def _():
            near_basis[i] = jnp.zeros(near_basis.shape[1:], F32)
            near_shift[i] = jnp.zeros(near_shift.shape[1:], F32)

        @pl.when(jnp.logical_not(have_y[i]))
        def _():
            near_basis[:, i] = jnp.zeros((3,) + near_basis.shape[2:], F32)
            near_shift[:, i] = jnp.zeros((3,) + near_shift.shape[2:], F32)

    for i in (0, 2):

        @pl.when(have_x[i])
        def _():
            pl.semaphore_signal(barrier, inc=1, device_id=(index_x + i - 1, index_y), device_id_type=pl.DeviceIdType.MESH)

        @pl.when(have_y[i])
        def _():
            pl.semaphore_signal(barrier, inc=1, device_id=(index_x, index_y + i - 1), device_id_type=pl.DeviceIdType.MESH)

        count += have_x[i].astype(jnp.int32) + have_y[i].astype(jnp.int32)
    pl.semaphore_wait(barrier, count)
    own = (bases.at[1], jitter.at[:, size:])
    near = (near_basis, near_shift)

    def along_x(i, part):
        return send(own[part], near[part].at[2 - i, 1], sends.at[0, i, 0, part], recvs.at[2 - i, 1, part], (index_x + i - 1, index_y))

    def along_y(i, k, part):
        source = own[part] if k == 1 else near[part].at[k, 1]
        return send(source, near[part].at[k, 2 - i], sends.at[1, i, k, part], recvs.at[k, 2 - i, part], (index_x, index_y + i - 1))

    def recv_wait(k, i, part):
        slot = near[part].at[k, i]
        send(slot, slot, sends.at[1, i, k, part], recvs.at[k, i, part], (index_x, index_y)).wait_recv()

    for i in (0, 2):

        @pl.when(have_x[i])
        def _():
            for part in (0, 1):
                along_x(i, part).start()

    for i in (0, 2):

        @pl.when(have_y[i])
        def _():
            for part in (0, 1):
                along_y(i, 1, part).start()

    near_basis[1, 1] = bases[1]
    near_shift[1, 1] = jitter[:, size:]
    table = table_ref[...]
    shifts = jitter[...]
    inner_x, inner_y = interior_points(shifts[:, :size], table)
    cycle_x, cycle_y = cycle_points(shifts[:, size:], table)
    inner_cx, inner_cy = column(inner_x), column(inner_y)
    cycle_cx, cycle_cy = column(cycle_x), column(cycle_y)
    eye = identity(size)
    basis_red, basis_skel = bases[0], bases[1]
    red_t, skel_t = basis_red.T, basis_skel.T

    kern_inner = wendland(inner_cx, inner_cy, inner_x, inner_y) + eye * noise[:, :size]
    rotated[0] = highest(red_t, highest(kern_inner, basis_red))
    for k in (0, 2):

        @pl.when(have_x[k])
        def _():
            for part in (0, 1):
                recv_wait(k, 1, part)

        for i in (0, 2):

            @pl.when(have_x[k] & have_y[i])
            def _():
                for part in (0, 1):
                    along_y(i, k, part).start()

    kern_mixed = wendland(inner_cx, inner_cy, cycle_x, cycle_y)
    rotated[1] = highest(red_t, highest(kern_mixed, basis_skel))
    kern_cycle = wendland(cycle_cx, cycle_cy, cycle_x, cycle_y) + eye * noise[:, size:]
    rotated[2] = highest(skel_t, highest(kern_cycle, basis_skel))

    for i in (0, 2):
        for k in (0, 1, 2):

            @pl.when(have_x[k] & have_y[i])
            def _():
                for part in (0, 1):
                    recv_wait(k, i, part)
                    along_y(i, k, part).wait_send()

        @pl.when(have_x[i])
        def _():
            for part in (0, 1):
                along_x(i, part).wait_send()


def box_kernel(rotated, factor, panel, schur):
    upper, rows = eliminate_block(rotated[0], rotated[1])
    factor[...] = upper.T
    panel[...] = rows
    schur[...] = rotated[2] - highest(rows.T, rows)


def flip(index, mask, bit):
    return index + bit * (mask - 2 * mask * (index // mask % 2))


def family(index_x, index_y, p):
    to_x = flip(flip(index_x, 2, p // 8), 1, p // 2 % 2)
    to_y = flip(flip(index_y, 2, p // 4 % 2), 1, p % 2)
    return to_x, to_y


def enter(devices):
    barrier = pltpu.get_barrier_semaphore()
    for device in devices:
        pl.semaphore_signal(barrier, inc=1, device_id=device, device_id_type=pl.DeviceIdType.MESH)
    pl.semaphore_wait(barrier, len(devices))


def coupling_kernel(jitter, bases, table_ref, near_basis, near_shift, schur, couplings, pairs, near, diag, cross, sends, recvs):
    size = bases.shape[-1]
    shed = size - size // 4
    index_x, index_y = place()
    child_x, child_y = index_x % 2, index_y % 2
    own_slot = 2 * child_x + child_y
    other_slot = 2 * (1 - child_x) + child_y
    tile_slot = 2 * (2 * (index_x // 2 % 2) + index_y // 2 % 2) + child_x
    boxes = {p: family(index_x, index_y, p) for p in (1, 2, 4, 6, 8, 10, 12, 14)}
    enter(list(boxes.values()))
    across = send(schur, diag.at[own_slot], sends.at[0], recvs.at[0], boxes[2])
    beside = send(schur, diag.at[own_slot], sends.at[1], recvs.at[1], boxes[1])
    onward = send(diag.at[other_slot], diag.at[other_slot], sends.at[3], recvs.at[3], boxes[1])
    across.start()
    beside.start()
    diag[own_slot] = schur[...]
    table = table_ref[...]
    cycle_x, cycle_y = cycle_points(jitter[:, size:], table)
    column_x, column_y = column(cycle_x), column(cycle_y)
    skel_t = bases[1].T

    def couple(n):
        step_x, step_y = OFFSETS[n]
        other_x, other_y = cycle_points(near_shift[1 + step_x, 1 + step_y], table)
        kern = wendland(column_x, column_y, step_x + other_x, step_y + other_y)
        block = highest(skel_t, highest(kern, near_basis[1 + step_x, 1 + step_y]))
        couplings[n] = block
        return block[shed:, shed:]

    tile = jnp.concatenate([couple(n) for n in range(4, 8)], axis=1)
    cross[...] = tile
    near[tile_slot] = tile
    for n in range(2):
        couple(n)
    tiles = [
        send(cross, near.at[tile_slot], sends.at[p], recvs.at[p], boxes[p])
        for p in (14, 12, 10, 8, 6, 4, 2)
    ]
    for copy in tiles:
        copy.start()
    for n in range(2, 4):
        couple(n)
    across.wait_recv()
    onward.start()
    sources = []
    for slot in range(4):
        at = (1 + slot // 2 - child_x, 1 + slot % 2 - child_y)
        sources.append((near_basis[at],) + cycle_points(near_shift[at], table))
    count = 0
    for slot in range(3):
        basis_t = sources[slot][0].T
        from_x, from_y = column(sources[slot][1]), column(sources[slot][2])
        for other in range(slot + 1, 4):
            basis, to_x, to_y = sources[other]
            step_x, step_y = other // 2 - slot // 2, other % 2 - slot % 2
            kern = wendland(from_x, from_y, step_x + to_x, step_y + to_y)
            pairs[count] = highest(basis_t, highest(kern, basis))
            count += 1
    across.wait_send()
    for copy in [beside, onward] + tiles:
        copy.wait()


def gather_kernel(schur, tiles, diag, near, sends, recvs, local):
    size = schur.shape[0]
    half = size // 2
    index_x, index_y = place()
    side = index_y % 2
    parent = 2 * (index_x // 2 % 2) + index_y // 2 % 2
    beside = family(index_x, index_y, 1)
    afar = [family(index_x, index_y, p) for p in (12, 8, 4)]
    mine = [
        pltpu.make_async_copy(schur, diag.at[parent], local.at[0]),
        pltpu.make_async_copy(tiles, near.at[side], local.at[1]),
    ]
    for copy in mine:
        copy.start()
    enter([beside] + afar)
    rows = pl.ds(pl.multiple_of(side * half, 8), half)
    out = [
        send(schur.at[rows], diag.at[parent, rows], sends.at[p], recvs.at[p], device)
        for p, device in enumerate(afar)
    ]
    for copy in out:
        copy.start()
    onward = [send(tiles, near.at[side], sends.at[3], recvs.at[3], beside)]
    onward[0].start()
    for p in range(3):
        other = (
            2 * ((index_x // 2 + (1, 1, 0)[p]) % 2) + (index_y // 2 + (1, 0, 1)[p]) % 2
        )
        out[p].wait_recv()
        block = diag.at[other, rows]
        onward.append(send(block, block, sends.at[4 + p], recvs.at[4 + p], beside))
        onward[-1].start()
    for copy in mine + onward:
        copy.wait()
    for copy in out:
        copy.wait_send()


def eliminate_large(shed_rows, kept_block, block, lower, panel_rows):
    size = shed_rows.shape[0]
    work = {
        i: shed_rows[i * block : (i + 1) * block, i * block :] for i in range(size // block)
    }
    for k in range(size // block):
        begin, end = k * block, (k + 1) * block
        upper, inverse = eliminate_block(work[k][:, :block], identity(block))
        rest = highest(inverse, work[k][:, block:])
        lower[begin:end, begin:end] = upper.T
        rest_t = rest.T
        for i in range(k + 1, size // block):
            part_t = rest_t[(i - k - 1) * block : (i - k) * block]
            work[i] = work[i] - highest(part_t, rest[:, (i - k - 1) * block :])
            lower[i * block : (i + 1) * block, begin:end] = part_t
            lower[begin:end, i * block : (i + 1) * block] = jnp.zeros((block, block), F32)
        tail = rest[:, size - end :]
        panel_rows[begin:end] = tail
        kept_block = kept_block - highest(rest_t[size - end :], tail)
    return kept_block


def split_rows(grid, shed):
    top = jnp.concatenate(
        [
            jnp.concatenate([b[:shed, :shed] for b in row] + [b[:shed, shed:] for b in row], axis=1)
            for row in grid
        ],
        axis=0,
    )
    kept = jnp.concatenate(
        [jnp.concatenate([b[shed:, shed:] for b in row], axis=1) for row in grid], axis=0
    )
    return top, kept


def parent_kernel(diag, pairs, factor, panel, schur, lower, panel_rows):
    size = pairs.shape[-1]
    shed = size - size // 4
    grid = [[None] * 4 for _ in range(4)]
    count = 0
    for slot in range(4):
        grid[slot][slot] = diag[slot]
        for other in range(slot + 1, 4):
            grid[slot][other] = pairs[count]
            grid[other][slot] = pairs[count].T
            count += 1
    rows, kept = split_rows(grid, shed)
    schur[...] = eliminate_large(rows, kept, size, lower, panel_rows)
    index_x, index_y = place()
    own = pl.ds(pl.multiple_of((2 * (index_x % 2) + index_y % 2) * shed, 8), shed)
    factor[...] = lower[own, :]
    panel[...] = panel_rows[own, :]


def grand_kernel(diag, near, factor, panel, schur, lower, panel_rows, kept_rows):
    size = diag.shape[-1]
    kept_size = size // 4
    shed = size - kept_size
    empty = jnp.zeros((kept_size, kept_size), F32)
    tiles = [near[g % 2, g // 2] for g in range(16)]
    turned = [tile.T for tile in tiles]

    def piece(e, c, f, d):
        gap_x = 2 * (f // 2 - e // 2) + d // 2 - c // 2
        gap_y = 2 * (f % 2 - e % 2) + d % 2 - c % 2
        if (gap_x, gap_y) in OFFSETS[4:]:
            at = OFFSETS[4:].index((gap_x, gap_y)) * kept_size
            return tiles[4 * e + c][:, at : at + kept_size]
        if (-gap_x, -gap_y) in OFFSETS[4:]:
            at = OFFSETS[4:].index((-gap_x, -gap_y)) * kept_size
            return turned[4 * f + d][at : at + kept_size]
        return empty

    grid = [[None] * 4 for _ in range(4)]
    for e in range(4):
        grid[e][e] = diag[e]
        for f in range(e + 1, 4):
            grid[e][f] = jnp.concatenate(
                [
                    jnp.concatenate([piece(e, c, f, d) for d in range(4)], axis=1)
                    for c in range(4)
                ],
                axis=0,
            )
            grid[f][e] = grid[e][f].T
    rows, kept = split_rows(grid, shed)
    kept_rows[...] = eliminate_large(rows, kept, size, lower, panel_rows)
    index_x, index_y = place()
    parent = 2 * (index_x // 2 % 2) + index_y // 2 % 2
    slot = 4 * parent + 2 * (index_x % 2) + index_y % 2

    def own(count):
        return pl.ds(pl.multiple_of(slot * count, 8), count)

    factor[...] = lower[own(shed // 4), :]
    panel[...] = panel_rows[own(shed // 4), :]
    schur[...] = kept_rows[own(size // 16), :]


def call(body, shapes, args, name, scratch=(), group=None):
    return pl.pallas_call(
        body,
        out_shape=[jax.ShapeDtypeStruct(s, F32) for s in shapes],
        in_specs=[pl.BlockSpec(memory_space=pltpu.VMEM)] * len(args),
        out_specs=[pl.BlockSpec(memory_space=pltpu.VMEM)] * len(shapes),
        scratch_shapes=[
            pltpu.SemaphoreType.DMA(s[1:]) if s[0] == 0 else pltpu.VMEM(s, F32) for s in scratch
        ],
        compiler_params=pltpu.CompilerParams(
            vmem_limit_bytes=48 * 2**20,
            collective_id=group,
            has_side_effects=group is not None,
        ),
        name=name,
    )(*args)


def on_device(jitter, noise_var, bases):
    jitter, noise, bases = jitter[0, 0], noise_var[0], bases[0, 0]
    size = bases.shape[-1]
    kept = size // 4
    shed = size - kept
    table = jnp.asarray(point_table(size))
    square = (size, size)
    rotated, near_basis, near_shift = call(
        front_kernel,
        [(3,) + square, (3, 3) + square, (3, 3, 2, size)],
        (jitter, noise, bases, table),
        "front",
        [(0, 2, 3, 3, 2), (0, 3, 3, 2)],
        group=0,
    )
    factor, panel, schur = call(box_kernel, [square] * 3, (rotated,), "box")
    couplings, pairs, tiles, quartet = call(
        coupling_kernel,
        [(8,) + square, (6,) + square, (8, kept, size), (4,) + square],
        (jitter, bases, table, near_basis, near_shift, schur),
        "coupling",
        [(kept, size), (0, 15), (0, 15)],
        group=1,
    )
    wide = 4 * shed
    parent_factor, parent_panel, parent_schur = call(
        parent_kernel,
        [(shed, wide), (shed, size), square],
        (quartet, pairs),
        "parent",
        [(wide, wide), (wide, size)],
    )
    upper, near = call(
        gather_kernel,
        [(4,) + square, (2, 8, kept, size)],
        (parent_schur, tiles),
        "gather",
        [(0, 7), (0, 7), (0, 2)],
        group=2,
    )
    top_factor, top_panel, top_schur = call(
        grand_kernel,
        [(shed // 4, wide), (shed // 4, size), (size // 16, size)],
        (upper, near),
        "grand",
        [(wide, wide), (wide, size), square],
    )
    outs = (
        factor,
        panel,
        couplings,
        parent_factor,
        parent_panel,
        top_factor,
        top_panel,
        top_schur,
    )
    return tuple(value[None, None] for value in outs)


def solution(mesh):
    spec4 = P("bx", "by", None, None)
    spec5 = P("bx", "by", None, None, None)
    return jax.shard_map(
        on_device,
        mesh=mesh,
        in_specs=(spec4, P("bx", "by", None), spec5),
        out_specs=(spec4, spec4, spec5, spec4, spec4, spec4, spec4, spec4),
        check_vma=False,
    )
```

profile of v0, /device:TPU:0, one launch (start us, length us, event | category | flops | bytes accessed | tf_op | source)
XLA Modules:
  0.0 61.6 jit_solution(7867334461690665207)
XLA Ops:
  0.6 0.0 copy-start.2
  0.6 0.0 copy-start.4
  0.7 0.7 %copy-done.2 = f32[8,128]{1,0:T(8,128)S(1)} copy-done((f32[8,128]{1,0:T(8,128)S(1)}, f32[8,128]{1,0:T(8,128)}, u32[]{:S(2)}) %copy-start.2) | copy-done | bytes 4120
  1.3 0.0 copy-done.4
  1.3 0.0 copy-start
  1.3 0.9 %copy-done = f32[1,1,2,128,128]{4,3,2,1,0:T(8,128)S(1)} copy-done((f32[1,1,2,128,128]{4,3,2,1,0:T(8,128)S(1)}, f32[1,1,2,128,128]{4,3,2,1,0:T(8,128)}, u32[]{:S(2)}) %copy-start) | copy-done | bytes 131096
  2.2 0.0 copy-start.3
  2.2 0.7 %copy-done.3 = f32[1,1,2,256]{3,2,1,0:T(2,128)S(1)} copy-done((f32[1,1,2,256]{3,2,1,0:T(2,128)S(1)}, f32[1,1,2,256]{3,2,1,0:T(2,128)}, u32[]{:S(2)}) %copy-start.3) | copy-done | bytes 2072
  2.9 8.4 %front.1 = (f32[3,128,128]{2,1,0:T(8,128)S(1)}, f32[3,3,128,128]{3,2,1,0:T(8,128)S(1)}, f32[3,3,2,128]{3,2,1,0:T(2,128)S(1)}) custom-call(f32[2,256]{1,0:T(2,128)S(1)} %bitcast.14, f32[1,256]{1,0:T(1,128)S(1)} %bitcast.16, f32[2,128,128]{2,1,0:T(8,128)S(1)} %bitcast.11, f32[8,128]{1,0:T(8,128)S(1)} %copy-done.2), custom_call_target="tpu_custom_call" | custom-call | tf_op jit(solution)/shard_map/front/pallas_call | solution.py:469
  11.3 0.0 copy-start.1
  11.3 4.5 %box.1 = (f32[128,128]{1,0:T(8,128)}, f32[128,128]{1,0:T(8,128)}, f32[128,128]{1,0:T(8,128)S(1)}) custom-call(f32[3,128,128]{2,1,0:T(8,128)S(1)} %get-tuple-element.26.rotated), custom_call_target="tpu_custom_call" | custom-call | tf_op jit(solution)/shard_map/box/pallas_call | solution.py:469
  15.8 0.0 copy-done.1
  15.8 10.6 %coupling.1 = (f32[8,128,128]{2,1,0:T(8,128)S(1)}, f32[6,128,128]{2,1,0:T(8,128)S(1)}, f32[8,32,128]{2,1,0:T(8,128)S(1)}, f32[4,128,128]{2,1,0:T(8,128)S(1)}) custom-call(f32[2,256]{1,0:T(2,128)S(1)} %bitcast.15, f32[2,128,128]{2,1,0:T(8,128)S(1)} %bitcast.12, f32[8,128]{1,0:T(8,128)S(1)} %copy-done.2, f32[3,3,128,128]{3,2,1,0:T(8,128)S(1)} %get-tuple-element.29.near_basis, ...), custom_call_target="tpu_custom_call" | custom-call | tf_op jit(solution)/shard_map/coupling/pallas_call | solution.py:469
  26.4 14.1 %parent.1 = (f32[96,384]{1,0:T(8,128)}, f32[96,128]{1,0:T(8,128)}, f32[128,128]{1,0:T(8,128)S(1)}) custom-call(f32[4,128,128]{2,1,0:T(8,128)S(1)} %get-tuple-element.33.diag, f32[6,128,128]{2,1,0:T(8,128)S(1)} %get-tuple-element.34.pairs), custom_call_target="tpu_custom_call" | custom-call | tf_op jit(solution)/shard_map/parent/pallas_call | solution.py:469
  40.5 6.2 %gather.1 = (f32[4,128,128]{2,1,0:T(8,128)S(1)}, f32[2,8,32,128]{3,2,1,0:T(8,128)S(1)}) custom-call(f32[128,128]{1,0:T(8,128)S(1)} %get-tuple-element.37.schur, f32[8,32,128]{2,1,0:T(8,128)S(1)} %get-tuple-element.38.tiles), custom_call_target="tpu_custom_call" | custom-call | tf_op jit(solution)/shard_map/gather/pallas_call | solution.py:469
  46.7 14.1 %grand.1 = (f32[24,384]{1,0:T(8,128)}, f32[24,128]{1,0:T(8,128)}, f32[8,128]{1,0:T(8,128)}) custom-call(f32[4,128,128]{2,1,0:T(8,128)S(1)} %get-tuple-element.39.diag, f32[2,8,32,128]{3,2,1,0:T(8,128)S(1)} %get-tuple-element.40.near), custom_call_target="tpu_custom_call" | custom-call | tf_op jit(solution)/shard_map/grand/pallas_call | solution.py:469
  60.8 0.8 %copy.13 = f32[1,1,8,128,128]{4,3,2,1,0:T(8,128)} copy(f32[1,1,8,128,128]{4,3,2,1,0:T(8,128)S(1)} %bitcast.13) | data formatting | bytes 1048576
Async XLA Ops:
  0.6 0.7 %copy-start.2 = (f32[8,128]{1,0:T(8,128)S(1)}, f32[8,128]{1,0:T(8,128)}, u32[]{:S(2)}) copy-start(f32[8,128]{1,0:T(8,128)} %constant.2.clone.table_ref) | copy-start | bytes 12292
  0.6 0.7 %copy-start.4 = (f32[1,1,256]{2,1,0:T(1,128)S(1)}, f32[1,1,256]{2,1,0:T(1,128)}, u32[]{:S(2)}) copy-start(f32[1,1,256]{2,1,0:T(1,128)} %param.5) | copy-start | bytes 3076
  1.3 0.9 %copy-start = (f32[1,1,2,128,128]{4,3,2,1,0:T(8,128)S(1)}, f32[1,1,2,128,128]{4,3,2,1,0:T(8,128)}, u32[]{:S(2)}) copy-start(f32[1,1,2,128,128]{4,3,2,1,0:T(8,128)} %param.6) | copy-start | bytes 393220
  2.2 0.7 %copy-start.3 = (f32[1,1,2,256]{3,2,1,0:T(2,128)S(1)}, f32[1,1,2,256]{3,2,1,0:T(2,128)}, u32[]{:S(2)}) copy-start(f32[1,1,2,256]{3,2,1,0:T(2,128)} %param.4) | copy-start | bytes 6148
  11.3 4.5 %copy-start.1 = (f32[1,1,2,128,128]{4,3,2,1,0:T(8,128)S(1)}, f32[1,1,2,128,128]{4,3,2,1,0:T(8,128)}, u32[]{:S(2)}) copy-start(f32[1,1,2,128,128]{4,3,2,1,0:T(8,128)} %param.6) | copy-start | bytes 393220
where the time goes:
time: 61.8 us; the launch traced here: 61.6 us
  Pallas kernels  57.9 us (94%)
  local copies, waits for them, and re-layouts  3.07 us (5%)
  between operations  0.69 us (1%)
    pallas_call x6, Pallas kernels, call(): pl.pallas_call(body, out_shape=[jax.ShapeDtypeStruct(s, F32) for s in sha...  57.9 us
    unnamed x11, local copies, waits for them, and re-layouts  3.07 us

commit v1 on v0

--- a/solution.py
+++ b/solution.py
@@ -327,44 +327,6 @@
         copy.wait()
 
 
-def gather_kernel(schur, tiles, diag, near, sends, recvs, local):
-    size = schur.shape[0]
-    half = size // 2
-    index_x, index_y = place()
-    side = index_y % 2
-    parent = 2 * (index_x // 2 % 2) + index_y // 2 % 2
-    beside = family(index_x, index_y, 1)
-    afar = [family(index_x, index_y, p) for p in (12, 8, 4)]
-    mine = [
-        pltpu.make_async_copy(schur, diag.at[parent], local.at[0]),
-        pltpu.make_async_copy(tiles, near.at[side], local.at[1]),
-    ]
-    for copy in mine:
-        copy.start()
-    enter([beside] + afar)
-    rows = pl.ds(pl.multiple_of(side * half, 8), half)
-    out = [
-        send(schur.at[rows], diag.at[parent, rows], sends.at[p], recvs.at[p], device)
-        for p, device in enumerate(afar)
-    ]
-    for copy in out:
-        copy.start()
-    onward = [send(tiles, near.at[side], sends.at[3], recvs.at[3], beside)]
-    onward[0].start()
-    for p in range(3):
-        other = (
-            2 * ((index_x // 2 + (1, 1, 0)[p]) % 2) + (index_y // 2 + (1, 0, 1)[p]) % 2
-        )
-        out[p].wait_recv()
-        block = diag.at[other, rows]
-        onward.append(send(block, block, sends.at[4 + p], recvs.at[4 + p], beside))
-        onward[-1].start()
-    for copy in mine + onward:
-        copy.wait()
-    for copy in out:
-        copy.wait_send()
-
-
 def eliminate_large(shed_rows, kept_block, block, lower, panel_rows):
     size = shed_rows.shape[0]
     work = {
@@ -401,9 +363,20 @@
     return top, kept
 
 
-def parent_kernel(diag, pairs, factor, panel, schur, lower, panel_rows):
+def parent_kernel(diag, pairs, tiles, factor, panel, upper, near, lower, panel_rows, schur, sends, recvs, local):
     size = pairs.shape[-1]
     shed = size - size // 4
+    half = size // 2
+    index_x, index_y = place()
+    side = index_y % 2
+    parent = 2 * (index_x // 2 % 2) + index_y // 2 % 2
+    beside = family(index_x, index_y, 1)
+    afar = [family(index_x, index_y, p) for p in (12, 8, 4)]
+    mine = pltpu.make_async_copy(tiles, near.at[side], local.at[0])
+    mine.start()
+    enter([beside] + afar)
+    onward = [send(tiles, near.at[side], sends.at[3], recvs.at[3], beside)]
+    onward[0].start()
     grid = [[None] * 4 for _ in range(4)]
     count = 0
     for slot in range(4):
@@ -413,11 +386,31 @@
             grid[other][slot] = pairs[count].T
             count += 1
     rows, kept = split_rows(grid, shed)
-    schur[...] = eliminate_large(rows, kept, size, lower, panel_rows)
-    index_x, index_y = place()
+    result = eliminate_large(rows, kept, size, lower, panel_rows)
+    schur[...] = result
+    upper[parent] = result
+    rows = pl.ds(pl.multiple_of(side * half, 8), half)
+    out = [
+        send(schur.at[rows], upper.at[parent, rows], sends.at[p], recvs.at[p], device)
+        for p, device in enumerate(afar)
+    ]
+    for copy in out:
+        copy.start()
     own = pl.ds(pl.multiple_of((2 * (index_x % 2) + index_y % 2) * shed, 8), shed)
     factor[...] = lower[own, :]
     panel[...] = panel_rows[own, :]
+    for p in range(3):
+        other = (
+            2 * ((index_x // 2 + (1, 1, 0)[p]) % 2) + (index_y // 2 + (1, 0, 1)[p]) % 2
+        )
+        out[p].wait_recv()
+        block = upper.at[other, rows]
+        onward.append(send(block, block, sends.at[4 + p], recvs.at[4 + p], beside))
+        onward[-1].start()
+    for copy in [mine] + onward:
+        copy.wait()
+    for copy in out:
+        copy.wait_send()
 
 
 def grand_kernel(diag, near, factor, panel, schur, lower, panel_rows, kept_rows):
@@ -508,19 +501,12 @@
         group=1,
     )
     wide = 4 * shed
-    parent_factor, parent_panel, parent_schur = call(
+    parent_factor, parent_panel, upper, near = call(
         parent_kernel,
-        [(shed, wide), (shed, size), square],
-        (quartet, pairs),
+        [(shed, wide), (shed, size), (4,) + square, (2, 8, kept, size)],
+        (quartet, pairs, tiles),
         "parent",
-        [(wide, wide), (wide, size)],
-    )
-    upper, near = call(
-        gather_kernel,
-        [(4,) + square, (2, 8, kept, size)],
-        (parent_schur, tiles),
-        "gather",
-        [(0, 7), (0, 7), (0, 2)],
+        [(wide, wide), (wide, size), square, (0, 7), (0, 7), (0, 1)],
         group=2,
     )
     top_factor, top_panel, top_schur = call(

time: 61.8 us -> 62.7 us (1.015)
  local copies, waits for them, and re-layouts: 3.07 us -> 4.35 us
    unnamed x11 -> x13, local copies, waits for them, and re-layouts: 3.07 us -> 4.35 us
    pallas_call x6 -> x5, Pallas kernels: 57.9 us -> 57.5 us  [call(): pl.pallas_call(body, out_shape=[jax.ShapeDtypeStruct(s, F32) for s in sha...]
where the time goes in v1:
time: 62.7 us; the launch traced here: 62.5 us
  Pallas kernels  57.5 us (92%)
  local copies, waits for them, and re-layouts  4.35 us (7%)
  between operations  0.69 us (1%)
    pallas_call x5, Pallas kernels, call(): pl.pallas_call(body, out_shape=[jax.ShapeDtypeStruct(s, F32) for s in sha...  57.5 us
    unnamed x13, local copies, waits for them, and re-layouts  4.35 us

profile of v1, /device:TPU:0, one launch (start us, length us, event | category | flops | bytes accessed | tf_op | source)
XLA Modules:
  0.0 62.5 jit_solution(7258415851182955914)
XLA Ops:
  0.6 0.0 copy-start.2
  0.6 0.0 copy-start.4
  0.7 0.7 %copy-done.2 = f32[8,128]{1,0:T(8,128)S(1)} copy-done((f32[8,128]{1,0:T(8,128)S(1)}, f32[8,128]{1,0:T(8,128)}, u32[]{:S(2)}) %copy-start.2) | copy-done | bytes 4120
  1.3 0.0 copy-done.4
  1.3 0.0 copy-start
  1.3 0.9 %copy-done = f32[1,1,2,128,128]{4,3,2,1,0:T(8,128)S(1)} copy-done((f32[1,1,2,128,128]{4,3,2,1,0:T(8,128)S(1)}, f32[1,1,2,128,128]{4,3,2,1,0:T(8,128)}, u32[]{:S(2)}) %copy-start) | copy-done | bytes 131096
  2.2 0.0 copy-start.3
  2.2 0.7 %copy-done.3 = f32[1,1,2,256]{3,2,1,0:T(2,128)S(1)} copy-done((f32[1,1,2,256]{3,2,1,0:T(2,128)S(1)}, f32[1,1,2,256]{3,2,1,0:T(2,128)}, u32[]{:S(2)}) %copy-start.3) | copy-done | bytes 2072
  2.9 8.4 %front.1 = (f32[3,128,128]{2,1,0:T(8,128)S(1)}, f32[3,3,128,128]{3,2,1,0:T(8,128)S(1)}, f32[3,3,2,128]{3,2,1,0:T(2,128)S(1)}) custom-call(f32[2,256]{1,0:T(2,128)S(1)} %bitcast.16, f32[1,256]{1,0:T(1,128)S(1)} %bitcast.18, f32[2,128,128]{2,1,0:T(8,128)S(1)} %bitcast.11, f32[8,128]{1,0:T(8,128)S(1)} %copy-done.2), custom_call_target="tpu_custom_call" | custom-call | tf_op jit(solution)/shard_map/front/pallas_call | solution.py:462
  11.3 0.0 copy-start.1
  11.3 4.5 %box.1 = (f32[128,128]{1,0:T(8,128)}, f32[128,128]{1,0:T(8,128)}, f32[128,128]{1,0:T(8,128)S(1)}) custom-call(f32[3,128,128]{2,1,0:T(8,128)S(1)} %get-tuple-element.25.rotated), custom_call_target="tpu_custom_call" | custom-call | tf_op jit(solution)/shard_map/box/pallas_call | solution.py:462
  15.8 0.0 copy-done.1
  15.8 10.6 %coupling.1 = (f32[8,128,128]{2,1,0:T(8,128)S(1)}, f32[6,128,128]{2,1,0:T(8,128)S(1)}, f32[8,32,128]{2,1,0:T(8,128)S(1)}, f32[4,128,128]{2,1,0:T(8,128)S(1)}) custom-call(f32[2,256]{1,0:T(2,128)S(1)} %bitcast.17, f32[2,128,128]{2,1,0:T(8,128)S(1)} %bitcast.12, f32[8,128]{1,0:T(8,128)S(1)} %copy-done.2, f32[3,3,128,128]{3,2,1,0:T(8,128)S(1)} %get-tuple-element.28.near_basis, ...), custom_call_target="tpu_custom_call" | custom-call | tf_op jit(solution)/shard_map/coupling/pallas_call | solution.py:462
  26.4 19.8 %parent.1 = (f32[96,384]{1,0:T(8,128)S(1)}, f32[96,128]{1,0:T(8,128)S(1)}, f32[4,128,128]{2,1,0:T(8,128)S(1)}, f32[2,8,32,128]{3,2,1,0:T(8,128)S(1)}) custom-call(f32[4,128,128]{2,1,0:T(8,128)S(1)} %get-tuple-element.32.diag, f32[6,128,128]{2,1,0:T(8,128)S(1)} %get-tuple-element.33.pairs, f32[8,32,128]{2,1,0:T(8,128)S(1)} %get-tuple-element.34.tiles), custom_call_target="tpu_custom_call" | custom-call | tf_op jit(solution)/shard_map/parent/pallas_call | solution.py:462
  46.2 14.3 %grand.1 = (f32[24,384]{1,0:T(8,128)}, f32[24,128]{1,0:T(8,128)}, f32[8,128]{1,0:T(8,128)}) custom-call(f32[4,128,128]{2,1,0:T(8,128)S(1)} %get-tuple-element.37.diag, f32[2,8,32,128]{3,2,1,0:T(8,128)S(1)} %get-tuple-element.38.near), custom_call_target="tpu_custom_call" | custom-call | tf_op jit(solution)/shard_map/grand/pallas_call | solution.py:462
  60.5 0.8 %copy.15 = f32[1,1,8,128,128]{4,3,2,1,0:T(8,128)} copy(f32[1,1,8,128,128]{4,3,2,1,0:T(8,128)S(1)} %bitcast.13) | data formatting | bytes 1048576
  61.3 0.7 %copy.16 = f32[1,1,96,384]{3,2,1,0:T(8,128)} copy(f32[1,1,96,384]{3,2,1,0:T(8,128)S(1)} %bitcast.14) | data formatting | bytes 294912
  61.9 0.6 copy.17
Async XLA Ops:
  0.6 0.7 %copy-start.2 = (f32[8,128]{1,0:T(8,128)S(1)}, f32[8,128]{1,0:T(8,128)}, u32[]{:S(2)}) copy-start(f32[8,128]{1,0:T(8,128)} %constant.2.clone.table_ref) | copy-start | bytes 12292
  0.6 0.7 %copy-start.4 = (f32[1,1,256]{2,1,0:T(1,128)S(1)}, f32[1,1,256]{2,1,0:T(1,128)}, u32[]{:S(2)}) copy-start(f32[1,1,256]{2,1,0:T(1,128)} %param.5) | copy-start | bytes 3076
  1.3 0.9 %copy-start = (f32[1,1,2,128,128]{4,3,2,1,0:T(8,128)S(1)}, f32[1,1,2,128,128]{4,3,2,1,0:T(8,128)}, u32[]{:S(2)}) copy-start(f32[1,1,2,128,128]{4,3,2,1,0:T(8,128)} %param.6) | copy-start | bytes 393220
  2.2 0.7 %copy-start.3 = (f32[1,1,2,256]{3,2,1,0:T(2,128)S(1)}, f32[1,1,2,256]{3,2,1,0:T(2,128)}, u32[]{:S(2)}) copy-start(f32[1,1,2,256]{3,2,1,0:T(2,128)} %param.4) | copy-start | bytes 6148
  11.3 4.5 %copy-start.1 = (f32[1,1,2,128,128]{4,3,2,1,0:T(8,128)S(1)}, f32[1,1,2,128,128]{4,3,2,1,0:T(8,128)}, u32[]{:S(2)}) copy-start(f32[1,1,2,128,128]{4,3,2,1,0:T(8,128)} %param.6) | copy-start | bytes 393220

commit v2 on v0

--- a/solution.py
+++ b/solution.py
@@ -10,63 +10,99 @@
 
 RIM = 0.125
 OFFSETS = ((-1, -1), (-1, 0), (-1, 1), (0, -1), (0, 1), (1, -1), (1, 0), (1, 1))
-PANEL = 64
+PANEL = 16
 F32 = jnp.float32
+BF16 = jnp.bfloat16
 
 
 def highest(left, right):
     return jnp.dot(left, right, precision=lax.Precision.HIGHEST, preferred_element_type=F32)
 
 
-def eliminate_block(block, rhs, panel=PANEL):
+def pieces(value):
+    high = value.astype(BF16)
+    rest = value - high.astype(F32)
+    middle = rest.astype(BF16)
+    return high, middle, (rest - middle.astype(F32)).astype(BF16)
+
+
+def joined(left, right, left_axis):
+    lh, lm, ll = pieces(left)
+    rh, rm, rl = pieces(right)
+    lefts = jnp.concatenate([lh, lh, lm, lm, lh, ll], axis=left_axis)
+    rights = jnp.concatenate([rh, rm, rh, rm, rl, rh], axis=0)
+    return (lefts if left_axis else lefts.T), rights
+
+
+def precise(left, right):
+    lefts, rights = joined(left, right, 1)
+    return jnp.dot(lefts, rights, preferred_element_type=F32)
+
+
+def precise_t(left_t, right):
+    lefts, rights = joined(left_t, right, 0)
+    return jnp.dot(lefts, rights, preferred_element_type=F32)
+
+
+def lane_copy(value, at):
+    return jnp.take_along_axis(
+        value, jnp.full(value.shape, at, jnp.int32), axis=1, mode="promise_in_bounds"
+    )
+
+
+def factor_block(block, panel=PANEL):
     size = block.shape[0]
-    rows_a = [block[8 * i : 8 * i + 8] for i in range(size // 8)]
-    rows_r = [rhs[8 * i : 8 * i + 8] for i in range(size // 8)]
-    sub = lax.broadcasted_iota(jnp.int32, rows_a[0].shape, 0)
+    rows = [block[8 * i : 8 * i + 8] for i in range(size // 8)]
+    sub = lax.broadcasted_iota(jnp.int32, rows[0].shape, 0)
+    lane = lax.broadcasted_iota(jnp.int32, rows[0].shape, 1)
+    uppers, diags = [], []
     for start in range(0, size, panel):
         stop = min(start + panel, size)
         first, last = start // 8, stop // 8
         for g in range(first, last):
             span = range(g, last)
-            cols = {
-                (m, i): jnp.broadcast_to(
-                    rows_a[i][:, 8 * g + m : 8 * g + m + 1], rows_a[i].shape
-                )
-                for i in span
-                for m in range(8)
-            }
+            cols = {(m, i): lane_copy(rows[i], 8 * g + m) for i in span for m in range(8)}
+            here = (lane >= 8 * g) & (lane < 8 * g + 8)
+            unit = jnp.where(sub == lane - 8 * g, 1.0, 0.0)
+            for i in span:
+                rows[i] = jnp.where(here, unit if i == g else 0.0, rows[i])
+            diag = jnp.zeros_like(rows[g])
             for j in range(8):
 
                 def row(value):
                     return jnp.broadcast_to(value[j : j + 1], value.shape)
 
                 inv = lax.rsqrt(row(cols[j, g]))
-                u_a = row(rows_a[g]) * inv
-                u_r = row(rows_r[g]) * inv
                 u_c = {m: row(cols[m, g]) * inv for m in range(j + 1, 8)}
+                mults = {}
                 for i in span:
-                    mult = cols[j, i] * inv
+                    mults[i] = cols[j, i] * inv
                     for m in range(j + 1, 8):
-                        cols[m, i] = cols[m, i] - mult * u_c[m]
-                    if i == g:
-                        below = jnp.where(sub > j, mult, 0.0)
-                        rows_a[i] = jnp.where(sub == j, u_a, rows_a[i] - below * u_a)
-                        rows_r[i] = jnp.where(sub == j, u_r, rows_r[i] - below * u_r)
-                    else:
-                        rows_a[i] = rows_a[i] - mult * u_a
-                        rows_r[i] = rows_r[i] - mult * u_r
+                        cols[m, i] = cols[m, i] - mults[i] * u_c[m]
+                u = row(rows[g]) * inv
+                diag = jnp.where((lane == 8 * g + j) & (sub >= j), mults[g], diag)
+                below = jnp.where(sub > j, mults[g], 0.0)
+                rows[g] = jnp.where(sub == j, u, rows[g] - below * u)
+                for i in span[1:]:
+                    rows[i] = rows[i] - mults[i] * u
+            diags.append(diag)
+            uppers.append(jnp.where(lane >= 8 * g + 8, rows[g], 0.0))
         if stop < size:
-            done_a = jnp.concatenate(rows_a[first:last], axis=0)
-            done_r = jnp.concatenate(rows_r[first:last], axis=0)
-            change = highest(done_a.T[stop:], jnp.concatenate([done_a, done_r], axis=1))
+            kept = [
+                jnp.where((lane >= 8 * g + 8) & (lane < stop), 0.0, rows[g])
+                for g in range(first, last)
+            ]
+            change = precise_t(
+                jnp.concatenate(uppers[first:last], axis=0), jnp.concatenate(kept, axis=0)
+            )
+            gone = (lane >= start) & (lane < stop)
             for i in range(last, size // 8):
-                off = 8 * i - stop
-                rows_a[i] = rows_a[i] - change[off : off + 8, :size]
-                rows_r[i] = rows_r[i] - change[off : off + 8, size:]
-    upper = jnp.concatenate(rows_a, axis=0)
-    row_id = lax.broadcasted_iota(jnp.int32, upper.shape, 0)
-    col_id = lax.broadcasted_iota(jnp.int32, upper.shape, 1)
-    return jnp.where(row_id <= col_id, upper, 0.0), jnp.concatenate(rows_r, axis=0)
+                rows[i] = jnp.where(gone, 0.0, rows[i]) - change[8 * i : 8 * i + 8]
+    lower = jnp.concatenate(uppers, axis=0).T + jnp.concatenate(diags, axis=0)
+    full = jnp.concatenate(rows, axis=0)
+    row_id = lax.broadcasted_iota(jnp.int32, full.shape, 0)
+    col_id = lax.broadcasted_iota(jnp.int32, full.shape, 1)
+    return lower, jnp.where(col_id < row_id // 8 * 8 + 8, full, 0.0)
 
 
 def identity(size):
@@ -241,10 +277,11 @@
 
 
 def box_kernel(rotated, factor, panel, schur):
-    upper, rows = eliminate_block(rotated[0], rotated[1])
-    factor[...] = upper.T
+    lower, inverse = factor_block(rotated[0])
+    rows = precise(inverse, rotated[1])
+    factor[...] = lower
     panel[...] = rows
-    schur[...] = rotated[2] - highest(rows.T, rows)
+    schur[...] = rotated[2] - precise(rows.T, rows)
 
 
 def flip(index, mask, bit):
@@ -372,18 +409,18 @@
     }
     for k in range(size // block):
         begin, end = k * block, (k + 1) * block
-        upper, inverse = eliminate_block(work[k][:, :block], identity(block))
-        rest = highest(inverse, work[k][:, block:])
-        lower[begin:end, begin:end] = upper.T
+        factor, inverse = factor_block(work[k][:, :block])
+        rest = precise(inverse, work[k][:, block:])
+        lower[begin:end, begin:end] = factor
         rest_t = rest.T
         for i in range(k + 1, size // block):
             part_t = rest_t[(i - k - 1) * block : (i - k) * block]
-            work[i] = work[i] - highest(part_t, rest[:, (i - k - 1) * block :])
+            work[i] = work[i] - precise(part_t, rest[:, (i - k - 1) * block :])
             lower[i * block : (i + 1) * block, begin:end] = part_t
             lower[begin:end, i * block : (i + 1) * block] = jnp.zeros((block, block), F32)
         tail = rest[:, size - end :]
         panel_rows[begin:end] = tail
-        kept_block = kept_block - highest(rest_t[size - end :], tail)
+        kept_block = kept_block - precise(rest_t[size - end :], tail)
     return kept_block
 
 

time: 61.8 us -> 60.5 us (0.979)
  Pallas kernels: 57.9 us -> 56.5 us
    pallas_call x6, Pallas kernels: 57.9 us -> 56.5 us  [call(): pl.pallas_call(body, out_shape=[jax.ShapeDtypeStruct(s, F32) for s in sha...]
where the time goes in v2:
time: 60.5 us; the launch traced here: 60.3 us
  Pallas kernels  56.5 us (93%)
  local copies, waits for them, and re-layouts  3.07 us (5%)
  between operations  0.69 us (1%)
    pallas_call x6, Pallas kernels, call(): pl.pallas_call(body, out_shape=[jax.ShapeDtypeStruct(s, F32) for s in sha...  56.5 us
    unnamed x11, local copies, waits for them, and re-layouts  3.07 us

profile of v2, /device:TPU:0, one launch (start us, length us, event | category | flops | bytes accessed | tf_op | source)
XLA Modules:
  0.0 60.3 jit_solution(1808459744883947109)
XLA Ops:
  0.6 0.0 copy-start.2
  0.6 0.0 copy-start.4
  0.7 0.7 %copy-done.2 = f32[8,128]{1,0:T(8,128)S(1)} copy-done((f32[8,128]{1,0:T(8,128)S(1)}, f32[8,128]{1,0:T(8,128)}, u32[]{:S(2)}) %copy-start.2) | copy-done | bytes 4120
  1.3 0.0 copy-done.4
  1.3 0.0 copy-start
  1.3 0.9 %copy-done = f32[1,1,2,128,128]{4,3,2,1,0:T(8,128)S(1)} copy-done((f32[1,1,2,128,128]{4,3,2,1,0:T(8,128)S(1)}, f32[1,1,2,128,128]{4,3,2,1,0:T(8,128)}, u32[]{:S(2)}) %copy-start) | copy-done | bytes 131096
  2.2 0.0 copy-start.3
  2.2 0.7 %copy-done.3 = f32[1,1,2,256]{3,2,1,0:T(2,128)S(1)} copy-done((f32[1,1,2,256]{3,2,1,0:T(2,128)S(1)}, f32[1,1,2,256]{3,2,1,0:T(2,128)}, u32[]{:S(2)}) %copy-start.3) | copy-done | bytes 2072
  2.9 8.4 %front.1 = (f32[3,128,128]{2,1,0:T(8,128)S(1)}, f32[3,3,128,128]{3,2,1,0:T(8,128)S(1)}, f32[3,3,2,128]{3,2,1,0:T(2,128)S(1)}) custom-call(f32[2,256]{1,0:T(2,128)S(1)} %bitcast.14, f32[1,256]{1,0:T(1,128)S(1)} %bitcast.16, f32[2,128,128]{2,1,0:T(8,128)S(1)} %bitcast.11, f32[8,128]{1,0:T(8,128)S(1)} %copy-done.2), custom_call_target="tpu_custom_call" | custom-call | tf_op jit(solution)/shard_map/front/pallas_call | solution.py:506
  11.3 0.0 copy-start.1
  11.3 4.4 %box.1 = (f32[128,128]{1,0:T(8,128)}, f32[128,128]{1,0:T(8,128)}, f32[128,128]{1,0:T(8,128)S(1)}) custom-call(f32[3,128,128]{2,1,0:T(8,128)S(1)} %get-tuple-element.26.rotated), custom_call_target="tpu_custom_call" | custom-call | tf_op jit(solution)/shard_map/box/pallas_call | solution.py:506
  15.7 0.0 copy-done.1
  15.7 10.6 %coupling.1 = (f32[8,128,128]{2,1,0:T(8,128)S(1)}, f32[6,128,128]{2,1,0:T(8,128)S(1)}, f32[8,32,128]{2,1,0:T(8,128)S(1)}, f32[4,128,128]{2,1,0:T(8,128)S(1)}) custom-call(f32[2,256]{1,0:T(2,128)S(1)} %bitcast.15, f32[2,128,128]{2,1,0:T(8,128)S(1)} %bitcast.12, f32[8,128]{1,0:T(8,128)S(1)} %copy-done.2, f32[3,3,128,128]{3,2,1,0:T(8,128)S(1)} %get-tuple-element.29.near_basis, ...), custom_call_target="tpu_custom_call" | custom-call | tf_op jit(solution)/shard_map/coupling/pallas_call | solution.py:506
  26.3 13.5 %parent.1 = (f32[96,384]{1,0:T(8,128)}, f32[96,128]{1,0:T(8,128)}, f32[128,128]{1,0:T(8,128)S(1)}) custom-call(f32[4,128,128]{2,1,0:T(8,128)S(1)} %get-tuple-element.33.diag, f32[6,128,128]{2,1,0:T(8,128)S(1)} %get-tuple-element.34.pairs), custom_call_target="tpu_custom_call" | custom-call | tf_op jit(solution)/shard_map/parent/pallas_call | solution.py:506
  39.8 6.2 %gather.1 = (f32[4,128,128]{2,1,0:T(8,128)S(1)}, f32[2,8,32,128]{3,2,1,0:T(8,128)S(1)}) custom-call(f32[128,128]{1,0:T(8,128)S(1)} %get-tuple-element.37.schur, f32[8,32,128]{2,1,0:T(8,128)S(1)} %get-tuple-element.38.tiles), custom_call_target="tpu_custom_call" | custom-call | tf_op jit(solution)/shard_map/gather/pallas_call | solution.py:506
  46.1 13.4 %grand.1 = (f32[24,384]{1,0:T(8,128)}, f32[24,128]{1,0:T(8,128)}, f32[8,128]{1,0:T(8,128)}) custom-call(f32[4,128,128]{2,1,0:T(8,128)S(1)} %get-tuple-element.39.diag, f32[2,8,32,128]{3,2,1,0:T(8,128)S(1)} %get-tuple-element.40.near), custom_call_target="tpu_custom_call" | custom-call | tf_op jit(solution)/shard_map/grand/pallas_call | solution.py:506
  59.5 0.8 %copy.13 = f32[1,1,8,128,128]{4,3,2,1,0:T(8,128)} copy(f32[1,1,8,128,128]{4,3,2,1,0:T(8,128)S(1)} %bitcast.13) | data formatting | bytes 1048576
Async XLA Ops:
  0.6 0.7 %copy-start.2 = (f32[8,128]{1,0:T(8,128)S(1)}, f32[8,128]{1,0:T(8,128)}, u32[]{:S(2)}) copy-start(f32[8,128]{1,0:T(8,128)} %constant.2.clone.table_ref) | copy-start | bytes 12292
  0.6 0.7 %copy-start.4 = (f32[1,1,256]{2,1,0:T(1,128)S(1)}, f32[1,1,256]{2,1,0:T(1,128)}, u32[]{:S(2)}) copy-start(f32[1,1,256]{2,1,0:T(1,128)} %param.5) | copy-start | bytes 3076
  1.3 0.9 %copy-start = (f32[1,1,2,128,128]{4,3,2,1,0:T(8,128)S(1)}, f32[1,1,2,128,128]{4,3,2,1,0:T(8,128)}, u32[]{:S(2)}) copy-start(f32[1,1,2,128,128]{4,3,2,1,0:T(8,128)} %param.6) | copy-start | bytes 393220
  2.2 0.7 %copy-start.3 = (f32[1,1,2,256]{3,2,1,0:T(2,128)S(1)}, f32[1,1,2,256]{3,2,1,0:T(2,128)}, u32[]{:S(2)}) copy-start(f32[1,1,2,256]{3,2,1,0:T(2,128)} %param.4) | copy-start | bytes 6148
  11.3 4.4 %copy-start.1 = (f32[1,1,2,128,128]{4,3,2,1,0:T(8,128)S(1)}, f32[1,1,2,128,128]{4,3,2,1,0:T(8,128)}, u32[]{:S(2)}) copy-start(f32[1,1,2,128,128]{4,3,2,1,0:T(8,128)} %param.6) | copy-start | bytes 393220

commit v3 on v2

--- a/solution.py
+++ b/solution.py
@@ -2,7 +2,6 @@
 
 import jax
 import jax.numpy as jnp
-import numpy as np
 from jax import lax
 from jax.experimental import pallas as pl
 from jax.experimental.pallas import tpu as pltpu
@@ -10,13 +9,9 @@
 
 RIM = 0.125
 OFFSETS = ((-1, -1), (-1, 0), (-1, 1), (0, -1), (0, 1), (1, -1), (1, 0), (1, 1))
-PANEL = 16
+PANEL = 64
 F32 = jnp.float32
 BF16 = jnp.bfloat16
-
-
-def highest(left, right):
-    return jnp.dot(left, right, precision=lax.Precision.HIGHEST, preferred_element_type=F32)
 
 
 def pieces(value):
@@ -112,29 +107,30 @@
 
 
 def point_table(count):
-    ids = np.arange(count)
+    ids = lax.broadcasted_iota(jnp.int32, (1, count), 1).astype(F32)
     side = 2 * math.isqrt(count // 2)
-    within = ids % (count // 4)
-    table = np.zeros((8, count), np.float32)
-    table[0] = ids // side
-    table[1] = ids % side
-    table[2] = within % (count // 8)
-    table[3] = within // (count // 8)
-    table[4] = ids // (count // 4)
-    return table
+
+    def quotient(value, by):
+        return jnp.floor((value + 0.5) / by)
+
+    lead = quotient(ids, side)
+    strip = quotient(ids, count // 4)
+    within = ids - strip * (count // 4)
+    layer = quotient(within, count // 8)
+    return (lead, ids - lead * side, within - layer * (count // 8), layer, strip)
 
 
 def interior_points(shifts, table):
     side = math.isqrt(shifts.shape[-1] // 2)
-    pos_x = RIM + (table[0:1] + shifts[0:1]) * ((1.0 - 2.0 * RIM) / side)
-    pos_y = RIM + (table[1:2] + shifts[1:2]) * ((1.0 - 2.0 * RIM) / (2 * side))
+    pos_x = RIM + (table[0] + shifts[0:1]) * ((1.0 - 2.0 * RIM) / side)
+    pos_y = RIM + (table[1] + shifts[1:2]) * ((1.0 - 2.0 * RIM) / (2 * side))
     return pos_x, pos_y
 
 
 def cycle_points(shifts, table):
-    along = (table[2:3] + shifts[0:1]) / (shifts.shape[-1] // 8)
-    depth = (table[3:4] + shifts[1:2]) * (0.5 * RIM)
-    strip = table[4:5]
+    along = (table[2] + shifts[0:1]) / (shifts.shape[-1] // 8)
+    depth = (table[3] + shifts[1:2]) * (0.5 * RIM)
+    strip = table[4]
     pos_x = jnp.where(strip == 2.0, depth, jnp.where(strip == 3.0, 1.0 - depth, along))
     pos_y = jnp.where(strip == 0.0, depth, jnp.where(strip == 1.0, 1.0 - depth, along))
     return pos_x, pos_y
@@ -168,8 +164,19 @@
     )
 
 
-def front_kernel(jitter, noise, bases, table_ref, rotated, near_basis, near_shift, sends, recvs):
-    size = bases.shape[-1]
+def front_kernel(
+    jitter_far, noise_far, bases_far, near_basis, near_shift, factor, panel, schur,
+    jitter, noise, basis_red_ref, sends, recvs, local,
+):
+    size = bases_far.shape[-1]
+    mine = [
+        pltpu.make_async_copy(jitter_far, jitter, local.at[0]),
+        pltpu.make_async_copy(noise_far, noise, local.at[1]),
+        pltpu.make_async_copy(bases_far.at[0], basis_red_ref, local.at[2]),
+        pltpu.make_async_copy(bases_far.at[1], near_basis.at[1, 1], local.at[3]),
+    ]
+    for copy in mine:
+        copy.start()
     index_x, index_y = place()
     last_x, last_y = lax.axis_size("bx") - 1, lax.axis_size("by") - 1
     have_x = {0: index_x > 0, 1: index_x >= 0, 2: index_x < last_x}
@@ -200,7 +207,10 @@
 
         count += have_x[i].astype(jnp.int32) + have_y[i].astype(jnp.int32)
     pl.semaphore_wait(barrier, count)
-    own = (bases.at[1], jitter.at[:, size:])
+    for copy in mine:
+        copy.wait()
+    near_shift[1, 1] = jitter[:, size:]
+    own = (near_basis.at[1, 1], near_shift.at[1, 1])
     near = (near_basis, near_shift)
 
     def along_x(i, part):
@@ -228,20 +238,22 @@
             for part in (0, 1):
                 along_y(i, 1, part).start()
 
-    near_basis[1, 1] = bases[1]
-    near_shift[1, 1] = jitter[:, size:]
-    table = table_ref[...]
+    table = point_table(size)
     shifts = jitter[...]
     inner_x, inner_y = interior_points(shifts[:, :size], table)
     cycle_x, cycle_y = cycle_points(shifts[:, size:], table)
     inner_cx, inner_cy = column(inner_x), column(inner_y)
     cycle_cx, cycle_cy = column(cycle_x), column(cycle_y)
     eye = identity(size)
-    basis_red, basis_skel = bases[0], bases[1]
+    basis_red, basis_skel = basis_red_ref[...], near_basis[1, 1]
     red_t, skel_t = basis_red.T, basis_skel.T
 
     kern_inner = wendland(inner_cx, inner_cy, inner_x, inner_y) + eye * noise[:, :size]
-    rotated[0] = highest(red_t, highest(kern_inner, basis_red))
+    kern_mixed = wendland(inner_cx, inner_cy, cycle_x, cycle_y)
+    kern_cycle = wendland(cycle_cx, cycle_cy, cycle_x, cycle_y) + eye * noise[:, size:]
+    block = precise(red_t, precise(kern_inner, basis_red))
+    mixed = precise(red_t, precise(kern_mixed, basis_skel))
+    cycle = precise(skel_t, precise(kern_cycle, basis_skel))
     for k in (0, 2):
 
         @pl.when(have_x[k])
@@ -256,10 +268,11 @@
                 for part in (0, 1):
                     along_y(i, k, part).start()
 
-    kern_mixed = wendland(inner_cx, inner_cy, cycle_x, cycle_y)
-    rotated[1] = highest(red_t, highest(kern_mixed, basis_skel))
-    kern_cycle = wendland(cycle_cx, cycle_cy, cycle_x, cycle_y) + eye * noise[:, size:]
-    rotated[2] = highest(skel_t, highest(kern_cycle, basis_skel))
+    lower, inverse = factor_block(block)
+    rows = precise(inverse, mixed)
+    factor[...] = lower
+    panel[...] = rows
+    schur[...] = cycle - precise(rows.T, rows)
 
     for i in (0, 2):
         for k in (0, 1, 2):
@@ -276,14 +289,6 @@
                 along_x(i, part).wait_send()
 
 
-def box_kernel(rotated, factor, panel, schur):
-    lower, inverse = factor_block(rotated[0])
-    rows = precise(inverse, rotated[1])
-    factor[...] = lower
-    panel[...] = rows
-    schur[...] = rotated[2] - precise(rows.T, rows)
-
-
 def flip(index, mask, bit):
     return index + bit * (mask - 2 * mask * (index // mask % 2))
 
@@ -301,15 +306,15 @@
     pl.semaphore_wait(barrier, len(devices))
 
 
-def coupling_kernel(jitter, bases, table_ref, near_basis, near_shift, schur, couplings, pairs, near, diag, cross, sends, recvs):
-    size = bases.shape[-1]
+def coupling_kernel(near_basis, near_shift, schur, couplings, pairs, near, diag, cross, sends, recvs):
+    size = near_basis.shape[-1]
     shed = size - size // 4
     index_x, index_y = place()
     child_x, child_y = index_x % 2, index_y % 2
     own_slot = 2 * child_x + child_y
     other_slot = 2 * (1 - child_x) + child_y
-    tile_slot = 2 * (2 * (index_x // 2 % 2) + index_y // 2 % 2) + child_x
-    boxes = {p: family(index_x, index_y, p) for p in (1, 2, 4, 6, 8, 10, 12, 14)}
+    tile_slot = 4 * (2 * (index_x // 2 % 2) + index_y // 2 % 2) + own_slot
+    boxes = {p: family(index_x, index_y, p) for p in range(1, 16)}
     enter(list(boxes.values()))
     across = send(schur, diag.at[own_slot], sends.at[0], recvs.at[0], boxes[2])
     beside = send(schur, diag.at[own_slot], sends.at[1], recvs.at[1], boxes[1])
@@ -317,16 +322,16 @@
     across.start()
     beside.start()
     diag[own_slot] = schur[...]
-    table = table_ref[...]
-    cycle_x, cycle_y = cycle_points(jitter[:, size:], table)
+    table = point_table(size)
+    cycle_x, cycle_y = cycle_points(near_shift[1, 1], table)
     column_x, column_y = column(cycle_x), column(cycle_y)
-    skel_t = bases[1].T
+    skel_t = near_basis[1, 1].T
 
     def couple(n):
         step_x, step_y = OFFSETS[n]
         other_x, other_y = cycle_points(near_shift[1 + step_x, 1 + step_y], table)
         kern = wendland(column_x, column_y, step_x + other_x, step_y + other_y)
-        block = highest(skel_t, highest(kern, near_basis[1 + step_x, 1 + step_y]))
+        block = precise(skel_t, precise(kern, near_basis[1 + step_x, 1 + step_y]))
         couplings[n] = block
         return block[shed:, shed:]
 
@@ -336,8 +341,8 @@
     for n in range(2):
         couple(n)
     tiles = [
-        send(cross, near.at[tile_slot], sends.at[p], recvs.at[p], boxes[p])
-        for p in (14, 12, 10, 8, 6, 4, 2)
+        send(cross, near.at[tile_slot], sends.at[3 + p], recvs.at[3 + p], boxes[p])
+        for p in range(15, 0, -1)
     ]
     for copy in tiles:
         copy.start()
@@ -357,14 +362,14 @@
             basis, to_x, to_y = sources[other]
             step_x, step_y = other // 2 - slot // 2, other % 2 - slot % 2
             kern = wendland(from_x, from_y, step_x + to_x, step_y + to_y)
-            pairs[count] = highest(basis_t, highest(kern, basis))
+            pairs[count] = precise(basis_t, precise(kern, basis))
             count += 1
     across.wait_send()
     for copy in [beside, onward] + tiles:
         copy.wait()
 
 
-def gather_kernel(schur, tiles, diag, near, sends, recvs, local):
+def gather_kernel(schur, diag, sends, recvs, local):
     size = schur.shape[0]
     half = size // 2
     index_x, index_y = place()
@@ -372,12 +377,8 @@
     parent = 2 * (index_x // 2 % 2) + index_y // 2 % 2
     beside = family(index_x, index_y, 1)
     afar = [family(index_x, index_y, p) for p in (12, 8, 4)]
-    mine = [
-        pltpu.make_async_copy(schur, diag.at[parent], local.at[0]),
-        pltpu.make_async_copy(tiles, near.at[side], local.at[1]),
-    ]
-    for copy in mine:
-        copy.start()
+    mine = pltpu.make_async_copy(schur, diag.at[parent], local.at[0])
+    mine.start()
     enter([beside] + afar)
     rows = pl.ds(pl.multiple_of(side * half, 8), half)
     out = [
@@ -386,17 +387,16 @@
     ]
     for copy in out:
         copy.start()
-    onward = [send(tiles, near.at[side], sends.at[3], recvs.at[3], beside)]
-    onward[0].start()
-    for p in range(3):
+    onward = []
+    for p in (2, 1, 0):
         other = (
             2 * ((index_x // 2 + (1, 1, 0)[p]) % 2) + (index_y // 2 + (1, 0, 1)[p]) % 2
         )
         out[p].wait_recv()
         block = diag.at[other, rows]
-        onward.append(send(block, block, sends.at[4 + p], recvs.at[4 + p], beside))
+        onward.append(send(block, block, sends.at[3 + p], recvs.at[3 + p], beside))
         onward[-1].start()
-    for copy in mine + onward:
+    for copy in [mine] + onward:
         copy.wait()
     for copy in out:
         copy.wait_send()
@@ -438,7 +438,18 @@
     return top, kept
 
 
-def parent_kernel(diag, pairs, factor, panel, schur, lower, panel_rows):
+def parent_kernel(
+    diag, pairs, held_factor, held_panel, held_couplings,
+    factor, panel, schur, box_factor, box_panel, couplings,
+    lower, panel_rows, local,
+):
+    out = [
+        pltpu.make_async_copy(held_factor, box_factor, local.at[0]),
+        pltpu.make_async_copy(held_panel, box_panel, local.at[1]),
+        pltpu.make_async_copy(held_couplings, couplings, local.at[2]),
+    ]
+    for copy in out:
+        copy.start()
     size = pairs.shape[-1]
     shed = size - size // 4
     grid = [[None] * 4 for _ in range(4)]
@@ -455,6 +466,8 @@
     own = pl.ds(pl.multiple_of((2 * (index_x % 2) + index_y % 2) * shed, 8), shed)
     factor[...] = lower[own, :]
     panel[...] = panel_rows[own, :]
+    for copy in out:
+        copy.wait()
 
 
 def grand_kernel(diag, near, factor, panel, schur, lower, panel_rows, kept_rows):
@@ -462,7 +475,7 @@
     kept_size = size // 4
     shed = size - kept_size
     empty = jnp.zeros((kept_size, kept_size), F32)
-    tiles = [near[g % 2, g // 2] for g in range(16)]
+    tiles = [near[g] for g in range(16)]
     turned = [tile.T for tile in tiles]
 
     def piece(e, c, f, d):
@@ -502,12 +515,15 @@
     schur[...] = kept_rows[own(size // 16), :]
 
 
-def call(body, shapes, args, name, scratch=(), group=None):
+def call(body, shapes, args, name, scratch=(), group=None, far=(), out_far=()):
+    def spec(far_away):
+        return pl.BlockSpec(memory_space=pltpu.HBM if far_away else pltpu.VMEM)
+
     return pl.pallas_call(
         body,
         out_shape=[jax.ShapeDtypeStruct(s, F32) for s in shapes],
-        in_specs=[pl.BlockSpec(memory_space=pltpu.VMEM)] * len(args),
-        out_specs=[pl.BlockSpec(memory_space=pltpu.VMEM)] * len(shapes),
+        in_specs=[spec(i in far) for i in range(len(args))],
+        out_specs=[spec(i in out_far) for i in range(len(shapes))],
         scratch_shapes=[
             pltpu.SemaphoreType.DMA(s[1:]) if s[0] == 0 else pltpu.VMEM(s, F32) for s in scratch
         ],
@@ -525,39 +541,39 @@
     size = bases.shape[-1]
     kept = size // 4
     shed = size - kept
-    table = jnp.asarray(point_table(size))
     square = (size, size)
-    rotated, near_basis, near_shift = call(
+    near_basis, near_shift, held_factor, held_panel, schur = call(
         front_kernel,
-        [(3,) + square, (3, 3) + square, (3, 3, 2, size)],
-        (jitter, noise, bases, table),
+        [(3, 3) + square, (3, 3, 2, size)] + [square] * 3,
+        (jitter, noise, bases),
         "front",
-        [(0, 2, 3, 3, 2), (0, 3, 3, 2)],
+        [jitter.shape, noise.shape, square, (0, 2, 3, 3, 2), (0, 3, 3, 2), (0, 4)],
         group=0,
-    )
-    factor, panel, schur = call(box_kernel, [square] * 3, (rotated,), "box")
-    couplings, pairs, tiles, quartet = call(
+        far=(0, 1, 2),
+    )
+    held_couplings, pairs, near, quartet = call(
         coupling_kernel,
-        [(8,) + square, (6,) + square, (8, kept, size), (4,) + square],
-        (jitter, bases, table, near_basis, near_shift, schur),
+        [(8,) + square, (6,) + square, (16, kept, size), (4,) + square],
+        (near_basis, near_shift, schur),
         "coupling",
-        [(kept, size), (0, 15), (0, 15)],
+        [(kept, size), (0, 19), (0, 19)],
         group=1,
     )
     wide = 4 * shed
-    parent_factor, parent_panel, parent_schur = call(
+    parent_factor, parent_panel, parent_schur, factor, panel, couplings = call(
         parent_kernel,
-        [(shed, wide), (shed, size), square],
-        (quartet, pairs),
+        [(shed, wide), (shed, size), square, square, square, (8,) + square],
+        (quartet, pairs, held_factor, held_panel, held_couplings),
         "parent",
-        [(wide, wide), (wide, size)],
-    )
-    upper, near = call(
+        [(wide, wide), (wide, size), (0, 3)],
+        out_far=(3, 4, 5),
+    )
+    (upper,) = call(
         gather_kernel,
-        [(4,) + square, (2, 8, kept, size)],
-        (parent_schur, tiles),
+        [(4,) + square],
+        (parent_schur,),
         "gather",
-        [(0, 7), (0, 7), (0, 2)],
+        [(0, 6), (0, 6), (0, 1)],
         group=2,
     )
     top_factor, top_panel, top_schur = call(

time: 60.5 us -> 57.2 us (0.945)
  Pallas kernels: 56.5 us -> 54.8 us
  local copies, waits for them, and re-layouts: 3.07 us -> 1.58 us
    pallas_call x6 -> x5, Pallas kernels: 56.5 us -> 54.8 us  [call(): pl.pallas_call(body, out_shape=[jax.ShapeDtypeStruct(s, F32) for s in sha...]
    unnamed x11 -> x6, local copies, waits for them, and re-layouts: 3.07 us -> 1.58 us
where the time goes in v3:
time: 57.2 us; the launch traced here: 57.1 us
  Pallas kernels  54.8 us (96%)
  local copies, waits for them, and re-layouts  1.58 us (3%)
  between operations  0.68 us (1%)
    pallas_call x5, Pallas kernels, call(): pl.pallas_call(body, out_shape=[jax.ShapeDtypeStruct(s, F32) for s in sha...  54.8 us
    unnamed x6, local copies, waits for them, and re-layouts  1.58 us

profile of v3, /device:TPU:0, one launch (start us, length us, event | category | flops | bytes accessed | tf_op | source)
XLA Modules:
  0.0 57.1 jit_solution(11657328740664267895)
XLA Ops:
  0.6 0.0 copy-start.1
  0.6 0.0 copy-start.2
  0.7 0.7 %copy-done.1 = f32[1,1,2,256]{3,2,1,0:T(2,128)S(1)} copy-done((f32[1,1,2,256]{3,2,1,0:T(2,128)S(1)}, f32[1,1,2,256]{3,2,1,0:T(2,128)}, u32[]{:S(2)}) %copy-start.1) | copy-done | bytes 2072
  1.3 0.0 copy-done.2
  1.3 0.0 copy-start
  1.3 0.9 %copy-done = f32[1,1,2,128,128]{4,3,2,1,0:T(8,128)S(1)} copy-done((f32[1,1,2,128,128]{4,3,2,1,0:T(8,128)S(1)}, f32[1,1,2,128,128]{4,3,2,1,0:T(8,128)}, u32[]{:S(2)}) %copy-start) | copy-done | bytes 131096
  2.2 11.5 %front.1 = (f32[3,3,128,128]{3,2,1,0:T(8,128)S(1)}, f32[3,3,2,128]{3,2,1,0:T(2,128)S(1)}, f32[128,128]{1,0:T(8,128)S(1)}, f32[128,128]{1,0:T(8,128)S(1)}, f32[128,128]{1,0:T(8,128)S(1)}) custom-call(f32[2,256]{1,0:T(2,128)S(1)} %bitcast.12, f32[1,256]{1,0:T(1,128)S(1)} %bitcast.13, f32[2,128,128]{2,1,0:T(8,128)S(1)} %bitcast.11), custom_call_target="tpu_custom_call" | custom-call | tf_op jit(solution)/shard_map/front/pallas_call | solution.py:522
  13.8 12.6 %coupling.1 = (f32[8,128,128]{2,1,0:T(8,128)S(1)}, f32[6,128,128]{2,1,0:T(8,128)S(1)}, f32[16,32,128]{2,1,0:T(8,128)S(1)}, f32[4,128,128]{2,1,0:T(8,128)S(1)}) custom-call(f32[3,3,128,128]{3,2,1,0:T(8,128)S(1)} %get-tuple-element.26.near_basis, f32[3,3,2,128]{3,2,1,0:T(2,128)S(1)} %get-tuple-element.27.near_shift, f32[128,128]{1,0:T(8,128)S(1)} %get-tuple-element.28.schur), custom_call_target="tpu_custom_call" | custom-call | tf_op jit(solution)/shard_map/coupling/pallas_call | solution.py:522
  26.4 12.9 %parent.1 = (f32[96,384]{1,0:T(8,128)}, f32[96,128]{1,0:T(8,128)}, f32[128,128]{1,0:T(8,128)S(1)}, f32[128,128]{1,0:T(8,128)}, f32[128,128]{1,0:T(8,128)}, /*index=5*/f32[8,128,128]{2,1,0:T(8,128)}) custom-call(f32[4,128,128]{2,1,0:T(8,128)S(1)} %get-tuple-element.29.diag, f32[6,128,128]{2,1,0:T(8,128)S(1)} %get-tuple-element.30.pairs, ...), custom_call_target="tpu_custom_call" | custom-call | tf_op jit(solution)/shard_map/parent/pallas_call | solution.py:522
  39.3 5.9 %gather.1.diag = f32[4,128,128]{2,1,0:T(8,128)S(1)} custom-call(f32[128,128]{1,0:T(8,128)S(1)} %get-tuple-element.39.schur), custom_call_target="tpu_custom_call" | custom-call | tf_op jit(solution)/shard_map/gather/pallas_call | solution.py:522
  45.2 11.9 %grand.1 = (f32[24,384]{1,0:T(8,128)}, f32[24,128]{1,0:T(8,128)}, f32[8,128]{1,0:T(8,128)}) custom-call(f32[4,128,128]{2,1,0:T(8,128)S(1)} %gather.1.diag, f32[16,32,128]{2,1,0:T(8,128)S(1)} %get-tuple-element.40.near), custom_call_target="tpu_custom_call" | custom-call | tf_op jit(solution)/shard_map/grand/pallas_call | solution.py:522
Async XLA Ops:
  0.6 0.7 %copy-start.1 = (f32[1,1,2,256]{3,2,1,0:T(2,128)S(1)}, f32[1,1,2,256]{3,2,1,0:T(2,128)}, u32[]{:S(2)}) copy-start(f32[1,1,2,256]{3,2,1,0:T(2,128)} %param.3) | copy-start | bytes 6148
  0.6 0.7 %copy-start.2 = (f32[1,1,256]{2,1,0:T(1,128)S(1)}, f32[1,1,256]{2,1,0:T(1,128)}, u32[]{:S(2)}) copy-start(f32[1,1,256]{2,1,0:T(1,128)} %param.4) | copy-start | bytes 3076
  1.3 0.9 %copy-start = (f32[1,1,2,128,128]{4,3,2,1,0:T(8,128)S(1)}, f32[1,1,2,128,128]{4,3,2,1,0:T(8,128)}, u32[]{:S(2)}) copy-start(f32[1,1,2,128,128]{4,3,2,1,0:T(8,128)} %param.5) | copy-start | bytes 393220

commit v4 on v3

--- a/solution.py
+++ b/solution.py
@@ -164,6 +164,20 @@
     )
 
 
+def facing(step_x, step_y):
+    high_x, high_y = int(step_x > 0), int(step_y > 0)
+    if step_y == 0:
+        return ((4 + 2 * high_x, 2, None), (0, 4, high_x))
+    if step_x == 0:
+        return ((2 * high_y, 2, None), (4, 4, high_y))
+    return ((2 * high_y, 2, high_x), (4 + 2 * high_x, 2, high_y))
+
+
+def some_rows(ref, part):
+    first, count, half = part
+    return ref.at[pl.ds(first, count)] if half is None else ref.at[pl.ds(first, count), half]
+
+
 def front_kernel(
     jitter_far, noise_far, bases_far, near_basis, near_shift, factor, panel, schur,
     jitter, noise, basis_red_ref, sends, recvs, local,
@@ -179,65 +193,83 @@
         copy.start()
     index_x, index_y = place()
     last_x, last_y = lax.axis_size("bx") - 1, lax.axis_size("by") - 1
-    have_x = {0: index_x > 0, 1: index_x >= 0, 2: index_x < last_x}
-    have_y = {0: index_y > 0, 2: index_y < last_y}
+    have_x = {-1: index_x > 0, 0: index_x >= 0, 1: index_x < last_x}
+    have_y = {-1: index_y > 0, 0: index_y >= 0, 1: index_y < last_y}
+    have = [have_x[o[0]] & have_y[o[1]] for o in OFFSETS]
+    whole = []
+    for step_x, step_y in OFFSETS:
+        if step_y == 0:
+            whole.append(index_x % 2 == int(step_x < 0))
+        elif step_x == 0:
+            whole.append(index_y % 2 == int(step_y < 0))
+        else:
+            whole.append(None)
+    for step_x, step_y in OFFSETS:
+        near_basis[1 + step_x, 1 + step_y] = jnp.zeros(near_basis.shape[2:], F32)
+        near_shift[1 + step_x, 1 + step_y] = jnp.zeros(near_shift.shape[2:], F32)
+    barrier = pltpu.get_barrier_semaphore()
     count = jnp.int32(0)
-    barrier = pltpu.get_barrier_semaphore()
-    for i in (0, 2):
-
-        @pl.when(jnp.logical_not(have_x[i]))
+    for n, (step_x, step_y) in enumerate(OFFSETS):
+
+        @pl.when(have[n])
         def _():
-            near_basis[i] = jnp.zeros(near_basis.shape[1:], F32)
-            near_shift[i] = jnp.zeros(near_shift.shape[1:], F32)
-
-        @pl.when(jnp.logical_not(have_y[i]))
-        def _():
-            near_basis[:, i] = jnp.zeros((3,) + near_basis.shape[2:], F32)
-            near_shift[:, i] = jnp.zeros((3,) + near_shift.shape[2:], F32)
-
-    for i in (0, 2):
-
-        @pl.when(have_x[i])
-        def _():
-            pl.semaphore_signal(barrier, inc=1, device_id=(index_x + i - 1, index_y), device_id_type=pl.DeviceIdType.MESH)
-
-        @pl.when(have_y[i])
-        def _():
-            pl.semaphore_signal(barrier, inc=1, device_id=(index_x, index_y + i - 1), device_id_type=pl.DeviceIdType.MESH)
-
-        count += have_x[i].astype(jnp.int32) + have_y[i].astype(jnp.int32)
-    pl.semaphore_wait(barrier, count)
+            pl.semaphore_signal(
+                barrier,
+                inc=1,
+                device_id=(index_x + step_x, index_y + step_y),
+                device_id_type=pl.DeviceIdType.MESH,
+            )
+
+        count += have[n].astype(jnp.int32)
     for copy in mine:
         copy.wait()
     near_shift[1, 1] = jitter[:, size:]
-    own = (near_basis.at[1, 1], near_shift.at[1, 1])
-    near = (near_basis, near_shift)
-
-    def along_x(i, part):
-        return send(own[part], near[part].at[2 - i, 1], sends.at[0, i, 0, part], recvs.at[2 - i, 1, part], (index_x + i - 1, index_y))
-
-    def along_y(i, k, part):
-        source = own[part] if k == 1 else near[part].at[k, 1]
-        return send(source, near[part].at[k, 2 - i], sends.at[1, i, k, part], recvs.at[k, 2 - i, part], (index_x, index_y + i - 1))
-
-    def recv_wait(k, i, part):
-        slot = near[part].at[k, i]
-        send(slot, slot, sends.at[1, i, k, part], recvs.at[k, i, part], (index_x, index_y)).wait_recv()
-
-    for i in (0, 2):
-
-        @pl.when(have_x[i])
-        def _():
-            for part in (0, 1):
-                along_x(i, part).start()
-
-    for i in (0, 2):
-
-        @pl.when(have_y[i])
-        def _():
-            for part in (0, 1):
-                along_y(i, 1, part).start()
-
+    pl.semaphore_wait(barrier, count)
+
+    def out(n, kind):
+        step_x, step_y = OFFSETS[n]
+        there = OFFSETS.index((-step_x, -step_y))
+        device = (index_x + step_x, index_y + step_y)
+        own, slot = near_basis.at[1, 1], near_basis.at[1 - step_x, 1 - step_y]
+        if kind == 3:
+            own, slot = near_shift.at[1, 1], near_shift.at[1 - step_x, 1 - step_y]
+        elif kind:
+            part = facing(step_x, step_y)[kind - 1]
+            own, slot = some_rows(own, part), some_rows(slot, part)
+        return send(own, slot, sends.at[n, kind], recvs.at[there, kind], device)
+
+    def come(n, kind):
+        step_x, step_y = OFFSETS[n]
+        slot = near_basis.at[1 + step_x, 1 + step_y]
+        if kind == 3:
+            slot = near_shift.at[1 + step_x, 1 + step_y]
+        elif kind:
+            slot = some_rows(slot, facing(-step_x, -step_y)[kind - 1])
+        device = (index_x + step_x, index_y + step_y)
+        return send(slot, slot, sends.at[n, kind], recvs.at[n, kind], device)
+
+    def each(n, act):
+        if whole[n] is None:
+
+            @pl.when(have[n])
+            def _():
+                for kind in (3, 1, 2):
+                    act(n, kind)
+
+        else:
+
+            @pl.when(have[n] & whole[n])
+            def _():
+                for kind in (3, 0):
+                    act(n, kind)
+
+            @pl.when(have[n] & jnp.logical_not(whole[n]))
+            def _():
+                for kind in (3, 1, 2):
+                    act(n, kind)
+
+    for n in (1, 6, 3, 4, 0, 2, 5, 7):
+        each(n, lambda n, kind: out(n, kind).start())
     table = point_table(size)
     shifts = jitter[...]
     inner_x, inner_y = interior_points(shifts[:, :size], table)
@@ -245,7 +277,9 @@
     inner_cx, inner_cy = column(inner_x), column(inner_y)
     cycle_cx, cycle_cy = column(cycle_x), column(cycle_y)
     eye = identity(size)
-    basis_red, basis_skel = basis_red_ref[...], near_basis[1, 1]
+    square = (size, size)
+    basis_red = basis_red_ref[...].reshape(square)
+    basis_skel = near_basis[1, 1].reshape(square)
     red_t, skel_t = basis_red.T, basis_skel.T
 
     kern_inner = wendland(inner_cx, inner_cy, inner_x, inner_y) + eye * noise[:, :size]
@@ -254,39 +288,18 @@
     block = precise(red_t, precise(kern_inner, basis_red))
     mixed = precise(red_t, precise(kern_mixed, basis_skel))
     cycle = precise(skel_t, precise(kern_cycle, basis_skel))
-    for k in (0, 2):
-
-        @pl.when(have_x[k])
-        def _():
-            for part in (0, 1):
-                recv_wait(k, 1, part)
-
-        for i in (0, 2):
-
-            @pl.when(have_x[k] & have_y[i])
-            def _():
-                for part in (0, 1):
-                    along_y(i, k, part).start()
-
     lower, inverse = factor_block(block)
     rows = precise(inverse, mixed)
     factor[...] = lower
     panel[...] = rows
     schur[...] = cycle - precise(rows.T, rows)
 
-    for i in (0, 2):
-        for k in (0, 1, 2):
-
-            @pl.when(have_x[k] & have_y[i])
-            def _():
-                for part in (0, 1):
-                    recv_wait(k, i, part)
-                    along_y(i, k, part).wait_send()
-
-        @pl.when(have_x[i])
-        def _():
-            for part in (0, 1):
-                along_x(i, part).wait_send()
+    def finish(n, kind):
+        come(n, kind).wait_recv()
+        out(n, kind).wait_send()
+
+    for n in range(8):
+        each(n, finish)
 
 
 def flip(index, mask, bit):
@@ -306,7 +319,7 @@
     pl.semaphore_wait(barrier, len(devices))
 
 
-def coupling_kernel(near_basis, near_shift, schur, couplings, pairs, near, diag, cross, sends, recvs):
+def coupling_kernel(near_basis, near_shift, schur, couplings, pairs, near, diag, cross, kin, sends, recvs):
     size = near_basis.shape[-1]
     shed = size - size // 4
     index_x, index_y = place()
@@ -319,8 +332,15 @@
     across = send(schur, diag.at[own_slot], sends.at[0], recvs.at[0], boxes[2])
     beside = send(schur, diag.at[own_slot], sends.at[1], recvs.at[1], boxes[1])
     onward = send(diag.at[other_slot], diag.at[other_slot], sends.at[3], recvs.at[3], boxes[1])
+    across_at = (2 - 2 * child_x, 1)
+    beside_at = (1, 2 - 2 * child_y)
+    relay = send(near_basis.at[across_at], kin.at[other_slot], sends.at[2], recvs.at[2], boxes[1])
     across.start()
     beside.start()
+    relay.start()
+    kin[own_slot] = near_basis[1, 1]
+    kin[2 * (1 - child_x) + child_y] = near_basis[across_at]
+    kin[2 * child_x + 1 - child_y] = near_basis[beside_at]
     diag[own_slot] = schur[...]
     table = point_table(size)
     cycle_x, cycle_y = cycle_points(near_shift[1, 1], table)
@@ -350,10 +370,11 @@
         couple(n)
     across.wait_recv()
     onward.start()
+    relay.wait()
     sources = []
     for slot in range(4):
         at = (1 + slot // 2 - child_x, 1 + slot % 2 - child_y)
-        sources.append((near_basis[at],) + cycle_points(near_shift[at], table))
+        sources.append((kin[slot],) + cycle_points(near_shift[at], table))
     count = 0
     for slot in range(3):
         basis_t = sources[slot][0].T
@@ -542,21 +563,22 @@
     kept = size // 4
     shed = size - kept
     square = (size, size)
+    strips = (8, 2, size // 16, size)
     near_basis, near_shift, held_factor, held_panel, schur = call(
         front_kernel,
-        [(3, 3) + square, (3, 3, 2, size)] + [square] * 3,
-        (jitter, noise, bases),
+        [(3, 3) + strips, (3, 3, 2, size)] + [square] * 3,
+        (jitter, noise, bases.reshape((2,) + strips)),
         "front",
-        [jitter.shape, noise.shape, square, (0, 2, 3, 3, 2), (0, 3, 3, 2), (0, 4)],
+        [jitter.shape, noise.shape, strips, (0, 8, 4), (0, 8, 4), (0, 4)],
         group=0,
         far=(0, 1, 2),
     )
     held_couplings, pairs, near, quartet = call(
         coupling_kernel,
         [(8,) + square, (6,) + square, (16, kept, size), (4,) + square],
-        (near_basis, near_shift, schur),
+        (near_basis.reshape((3, 3) + square), near_shift, schur),
         "coupling",
-        [(kept, size), (0, 19), (0, 19)],
+        [(kept, size), (4,) + square, (0, 19), (0, 19)],
         group=1,
     )
     wide = 4 * shed

time: 57.2 us -> 52.6 us (0.920)
  Pallas kernels: 54.8 us -> 50.2 us
    pallas_call x5, Pallas kernels: 54.8 us -> 50.2 us  [call(): pl.pallas_call(body, out_shape=[jax.ShapeDtypeStruct(s, F32) for s in sha...]
where the time goes in v4:
time: 52.6 us; the launch traced here: 52.5 us
  Pallas kernels  50.2 us (95%)
  local copies, waits for them, and re-layouts  1.58 us (3%)
  between operations  0.68 us (1%)
    pallas_call x5, Pallas kernels, call(): pl.pallas_call(body, out_shape=[jax.ShapeDtypeStruct(s, F32) for s in sha...  50.2 us
    unnamed x6, local copies, waits for them, and re-layouts  1.58 us

profile of v4, /device:TPU:0, one launch (start us, length us, event | category | flops | bytes accessed | tf_op | source)
XLA Modules:
  0.0 52.5 jit_solution(17559673167374567303)
XLA Ops:
  0.6 0.0 copy-start.1
  0.6 0.0 copy-start.2
  0.7 0.7 %copy-done.1 = f32[1,1,2,256]{3,2,1,0:T(2,128)S(1)} copy-done((f32[1,1,2,256]{3,2,1,0:T(2,128)S(1)}, f32[1,1,2,256]{3,2,1,0:T(2,128)}, u32[]{:S(2)}) %copy-start.1) | copy-done | bytes 2072
  1.3 0.0 copy-done.2
  1.3 0.0 copy-start
  1.3 0.9 %copy-done = f32[1,1,2,128,128]{4,3,2,1,0:T(8,128)S(1)} copy-done((f32[1,1,2,128,128]{4,3,2,1,0:T(8,128)S(1)}, f32[1,1,2,128,128]{4,3,2,1,0:T(8,128)}, u32[]{:S(2)}) %copy-start) | copy-done | bytes 131096
  2.2 8.8 %front.1 = (f32[3,3,8,2,8,128]{5,4,3,2,1,0:T(8,128)S(1)}, f32[3,3,2,128]{3,2,1,0:T(2,128)S(1)}, f32[128,128]{1,0:T(8,128)S(1)}, f32[128,128]{1,0:T(8,128)S(1)}, f32[128,128]{1,0:T(8,128)S(1)}) custom-call(f32[2,256]{1,0:T(2,128)S(1)} %bitcast.14, f32[1,256]{1,0:T(1,128)S(1)} %bitcast.15, f32[2,8,2,8,128]{4,3,2,1,0:T(8,128)S(1)} %bitcast.13), custom_call_target="tpu_custom_call" | custom-call | tf_op jit(solution)/shard_map/front/pallas_call | solution.py:543
  11.1 10.7 %coupling.1 = (f32[8,128,128]{2,1,0:T(8,128)S(1)}, f32[6,128,128]{2,1,0:T(8,128)S(1)}, f32[16,32,128]{2,1,0:T(8,128)S(1)}, f32[4,128,128]{2,1,0:T(8,128)S(1)}) custom-call(f32[3,3,128,128]{3,2,1,0:T(8,128)S(1)} %bitcast.12, f32[3,3,2,128]{3,2,1,0:T(2,128)S(1)} %get-tuple-element.27.near_shift, f32[128,128]{1,0:T(8,128)S(1)} %get-tuple-element.28.schur), custom_call_target="tpu_custom_call" | custom-call | tf_op jit(solution)/shard_map/coupling/pallas_call | solution.py:543
  21.8 12.9 %parent.1 = (f32[96,384]{1,0:T(8,128)}, f32[96,128]{1,0:T(8,128)}, f32[128,128]{1,0:T(8,128)S(1)}, f32[128,128]{1,0:T(8,128)}, f32[128,128]{1,0:T(8,128)}, /*index=5*/f32[8,128,128]{2,1,0:T(8,128)}) custom-call(f32[4,128,128]{2,1,0:T(8,128)S(1)} %get-tuple-element.29.diag, f32[6,128,128]{2,1,0:T(8,128)S(1)} %get-tuple-element.30.pairs, ...), custom_call_target="tpu_custom_call" | custom-call | tf_op jit(solution)/shard_map/parent/pallas_call | solution.py:543
  34.7 5.9 %gather.1.diag = f32[4,128,128]{2,1,0:T(8,128)S(1)} custom-call(f32[128,128]{1,0:T(8,128)S(1)} %get-tuple-element.39.schur), custom_call_target="tpu_custom_call" | custom-call | tf_op jit(solution)/shard_map/gather/pallas_call | solution.py:543
  40.6 11.9 %grand.1 = (f32[24,384]{1,0:T(8,128)}, f32[24,128]{1,0:T(8,128)}, f32[8,128]{1,0:T(8,128)}) custom-call(f32[4,128,128]{2,1,0:T(8,128)S(1)} %gather.1.diag, f32[16,32,128]{2,1,0:T(8,128)S(1)} %get-tuple-element.40.near), custom_call_target="tpu_custom_call" | custom-call | tf_op jit(solution)/shard_map/grand/pallas_call | solution.py:543
Async XLA Ops:
  0.6 0.7 %copy-start.1 = (f32[1,1,2,256]{3,2,1,0:T(2,128)S(1)}, f32[1,1,2,256]{3,2,1,0:T(2,128)}, u32[]{:S(2)}) copy-start(f32[1,1,2,256]{3,2,1,0:T(2,128)} %param.3) | copy-start | bytes 6148
  0.6 0.7 %copy-start.2 = (f32[1,1,256]{2,1,0:T(1,128)S(1)}, f32[1,1,256]{2,1,0:T(1,128)}, u32[]{:S(2)}) copy-start(f32[1,1,256]{2,1,0:T(1,128)} %param.4) | copy-start | bytes 3076
  1.3 0.9 %copy-start = (f32[1,1,2,128,128]{4,3,2,1,0:T(8,128)S(1)}, f32[1,1,2,128,128]{4,3,2,1,0:T(8,128)}, u32[]{:S(2)}) copy-start(f32[1,1,2,128,128]{4,3,2,1,0:T(8,128)} %param.5) | copy-start | bytes 393220

commit v5 on v4

--- a/solution.py
+++ b/solution.py
@@ -338,7 +338,6 @@
     across.start()
     beside.start()
     relay.start()
-    kin[own_slot] = near_basis[1, 1]
     kin[2 * (1 - child_x) + child_y] = near_basis[across_at]
     kin[2 * child_x + 1 - child_y] = near_basis[beside_at]
     diag[own_slot] = schur[...]
@@ -371,20 +370,29 @@
     across.wait_recv()
     onward.start()
     relay.wait()
-    sources = []
-    for slot in range(4):
-        at = (1 + slot // 2 - child_x, 1 + slot % 2 - child_y)
-        sources.append((kin[slot],) + cycle_points(near_shift[at], table))
-    count = 0
-    for slot in range(3):
-        basis_t = sources[slot][0].T
-        from_x, from_y = column(sources[slot][1]), column(sources[slot][2])
-        for other in range(slot + 1, 4):
-            basis, to_x, to_y = sources[other]
-            step_x, step_y = other // 2 - slot // 2, other % 2 - slot % 2
-            kern = wendland(from_x, from_y, step_x + to_x, step_y + to_y)
-            pairs[count] = precise(basis_t, precise(kern, basis))
-            count += 1
+    cross_y = child_x * child_y + (1 - child_x) * (1 - child_y)
+    mixed_y = 1 - cross_y
+    others = (
+        ((0, cross_y), (1, 1 - cross_y), 2 + cross_y),
+        ((0, 1 - child_y), (1, 1 - child_y), 4 - 3 * child_y),
+        ((1 - child_x, 0), (1 - child_x, 1), 5 - 5 * child_x),
+    )
+    for (low_x, low_y), (high_x, high_y), at in others:
+        low_points = cycle_points(near_shift[1 + low_x - child_x, 1 + low_y - child_y], table)
+        to_x, to_y = cycle_points(near_shift[1 + high_x - child_x, 1 + high_y - child_y], table)
+        step_x = jnp.asarray(high_x - low_x).astype(F32)
+        step_y = jnp.asarray(high_y - low_y).astype(F32)
+        kern = wendland(column(low_points[0]), column(low_points[1]), step_x + to_x, step_y + to_y)
+        basis_t = kin[2 * low_x + low_y].T
+        pairs[at] = precise(basis_t, precise(kern, kin[2 * high_x + high_y]))
+    mine = (
+        (4 - child_y, child_y == 0, 5 * child_x),
+        (6 - 5 * child_x, child_x == 0, 1 + 3 * child_y),
+        (7 - 5 * child_x - 2 * child_y, child_x == 0, 2 + mixed_y),
+    )
+    for n, leads, at in mine:
+        block = couplings[n]
+        pairs[at] = jnp.where(leads, block, block.T)
     across.wait_send()
     for copy in [beside, onward] + tiles:
         copy.wait()

time: 52.6 us -> 52.6 us (level)
  no operation moved by 1% of the time
where the time goes in v5:
time: 52.6 us; the launch traced here: 52.4 us
  Pallas kernels  50.2 us (95%)
  local copies, waits for them, and re-layouts  1.58 us (3%)
  between operations  0.68 us (1%)
    pallas_call x5, Pallas kernels, call(): pl.pallas_call(body, out_shape=[jax.ShapeDtypeStruct(s, F32) for s in sha...  50.2 us
    unnamed x6, local copies, waits for them, and re-layouts  1.58 us

profile of v5, /device:TPU:0, one launch (start us, length us, event | category | flops | bytes accessed | tf_op | source)
XLA Modules:
  0.0 52.4 jit_solution(5039628432969130953)
XLA Ops:
  0.6 0.0 copy-start.1
  0.6 0.0 copy-start.2
  0.7 0.7 %copy-done.1 = f32[1,1,2,256]{3,2,1,0:T(2,128)S(1)} copy-done((f32[1,1,2,256]{3,2,1,0:T(2,128)S(1)}, f32[1,1,2,256]{3,2,1,0:T(2,128)}, u32[]{:S(2)}) %copy-start.1) | copy-done | bytes 2072
  1.3 0.0 copy-done.2
  1.3 0.0 copy-start
  1.3 0.9 %copy-done = f32[1,1,2,128,128]{4,3,2,1,0:T(8,128)S(1)} copy-done((f32[1,1,2,128,128]{4,3,2,1,0:T(8,128)S(1)}, f32[1,1,2,128,128]{4,3,2,1,0:T(8,128)}, u32[]{:S(2)}) %copy-start) | copy-done | bytes 131096
  2.2 8.8 %front.1 = (f32[3,3,8,2,8,128]{5,4,3,2,1,0:T(8,128)S(1)}, f32[3,3,2,128]{3,2,1,0:T(2,128)S(1)}, f32[128,128]{1,0:T(8,128)S(1)}, f32[128,128]{1,0:T(8,128)S(1)}, f32[128,128]{1,0:T(8,128)S(1)}) custom-call(f32[2,256]{1,0:T(2,128)S(1)} %bitcast.14, f32[1,256]{1,0:T(1,128)S(1)} %bitcast.15, f32[2,8,2,8,128]{4,3,2,1,0:T(8,128)S(1)} %bitcast.13), custom_call_target="tpu_custom_call" | custom-call | tf_op jit(solution)/shard_map/front/pallas_call | solution.py:551
  11.1 10.7 %coupling.1 = (f32[8,128,128]{2,1,0:T(8,128)S(1)}, f32[6,128,128]{2,1,0:T(8,128)S(1)}, f32[16,32,128]{2,1,0:T(8,128)S(1)}, f32[4,128,128]{2,1,0:T(8,128)S(1)}) custom-call(f32[3,3,128,128]{3,2,1,0:T(8,128)S(1)} %bitcast.12, f32[3,3,2,128]{3,2,1,0:T(2,128)S(1)} %get-tuple-element.27.near_shift, f32[128,128]{1,0:T(8,128)S(1)} %get-tuple-element.28.schur), custom_call_target="tpu_custom_call" | custom-call | tf_op jit(solution)/shard_map/coupling/pallas_call | solution.py:551
  21.8 12.8 %parent.1 = (f32[96,384]{1,0:T(8,128)}, f32[96,128]{1,0:T(8,128)}, f32[128,128]{1,0:T(8,128)S(1)}, f32[128,128]{1,0:T(8,128)}, f32[128,128]{1,0:T(8,128)}, /*index=5*/f32[8,128,128]{2,1,0:T(8,128)}) custom-call(f32[4,128,128]{2,1,0:T(8,128)S(1)} %get-tuple-element.29.diag, f32[6,128,128]{2,1,0:T(8,128)S(1)} %get-tuple-element.30.pairs, ...), custom_call_target="tpu_custom_call" | custom-call | tf_op jit(solution)/shard_map/parent/pallas_call | solution.py:551
  34.6 5.9 %gather.1.diag = f32[4,128,128]{2,1,0:T(8,128)S(1)} custom-call(f32[128,128]{1,0:T(8,128)S(1)} %get-tuple-element.39.schur), custom_call_target="tpu_custom_call" | custom-call | tf_op jit(solution)/shard_map/gather/pallas_call | solution.py:551
  40.5 11.9 %grand.1 = (f32[24,384]{1,0:T(8,128)}, f32[24,128]{1,0:T(8,128)}, f32[8,128]{1,0:T(8,128)}) custom-call(f32[4,128,128]{2,1,0:T(8,128)S(1)} %gather.1.diag, f32[16,32,128]{2,1,0:T(8,128)S(1)} %get-tuple-element.40.near), custom_call_target="tpu_custom_call" | custom-call | tf_op jit(solution)/shard_map/grand/pallas_call | solution.py:551
Async XLA Ops:
  0.6 0.7 %copy-start.1 = (f32[1,1,2,256]{3,2,1,0:T(2,128)S(1)}, f32[1,1,2,256]{3,2,1,0:T(2,128)}, u32[]{:S(2)}) copy-start(f32[1,1,2,256]{3,2,1,0:T(2,128)} %param.3) | copy-start | bytes 6148
  0.6 0.7 %copy-start.2 = (f32[1,1,256]{2,1,0:T(1,128)S(1)}, f32[1,1,256]{2,1,0:T(1,128)}, u32[]{:S(2)}) copy-start(f32[1,1,256]{2,1,0:T(1,128)} %param.4) | copy-start | bytes 3076
  1.3 0.9 %copy-start = (f32[1,1,2,128,128]{4,3,2,1,0:T(8,128)S(1)}, f32[1,1,2,128,128]{4,3,2,1,0:T(8,128)}, u32[]{:S(2)}) copy-start(f32[1,1,2,128,128]{4,3,2,1,0:T(8,128)} %param.5) | copy-start | bytes 393220
